TPU v7x, 32 devices: a whole 2x2x4 slice. The times are simulated.
32 devices in a mesh: ctx: 4 (over z), pipe: 2 (over x), tp: 4 (over y, core).
Axes of the slice: x: 2, y: 2, z: 4, core: 2. Of those that a mesh axis runs over, the one named last changes fastest.
Arguments:
- upstream: bfloat16 [2, 512, 2688], P('pipe', 'ctx', 'tp'), may hold values from -6 to 6
- saved_input: bfloat16 [2, 512, 2688], P('pipe', 'ctx', 'tp'), may hold values from -0.59765625 to 0.59765625
- inv_rms: float32 [2, 512], P('pipe', 'ctx'), may hold values from 2 to 20
- norm_gain: float32 [2, 2688], P('pipe', 'tp'), may hold values from 0.1 to 1.9
- query_proj: bfloat16 [2, 512, 2048], P('pipe', 'ctx', 'tp'), may hold values from -14 to 14
- key_proj: bfloat16 [2, 512, 1024], P('pipe', 'ctx', 'tp'), may hold values from -5.2 to 5.2
- stored_value_rows: bfloat16 [2, 512, 1024], P('pipe', 'ctx', 'tp'), may hold values from -6 to 6
- attn_out: bfloat16 [2, 512, 2048], P('pipe', 'ctx', 'tp'), may hold values from -6 to 6
- w_query: bfloat16 [2, 2688, 2048], P('pipe', None, 'tp'), may hold values from -0.125 to 0.125
- key_projection_weight: bfloat16 [2, 2688, 1024], P('pipe', None, 'tp'), may hold values from -0.125 to 0.125
- value_projection_weight: bfloat16 [2, 2688, 1024], P('pipe', None, 'tp'), may hold values from -0.125 to 0.125
- w_out: bfloat16 [2, 2048, 2688], P('pipe', 'tp'), may hold values from -0.125 to 0.125
- seq_lengths: int32 [2], P('pipe'), may hold values from 256 to 512, as said below
Outputs:
- next_grad: bfloat16 [2, 512, 2688], P('pipe', 'ctx', 'tp')
Inputs may be any that keep to these rules, and one draw needn't show every extreme that they name: `seq_lengths`: valid tokens come first in each sequence; at least one section's sequence has all 512 tokens valid.
All inputs are finite; a program needn't handle non-finite values.
Results may differ from a plain program's by a relative error of at most 0.0062.
Values may be sent and summed in bfloat16 or wider, within the bound.
A program may use at most 64 MiB of HBM per device.

v0:
```python
import functools

import jax
import jax.numpy as jnp
from jax import lax
from jax.experimental import pallas as pl
from jax.experimental.pallas import tpu as pltpu
from jax.sharding import PartitionSpec as P

QUERY_HEADS = 16
KEY_VALUE_HEADS = 8
HEAD_SIZE = 128
WINDOW = 1024
QUERY_SCALAR = 168
NEG_FILL = -1e30
GATHER_PARTS = 2
COUPLING_ROWS = 16
NT = (((1,), (1,)), ((), ()))
NN = (((1,), (0,)), ((), ()))
TN = (((0,), (0,)), ((), ()))
BF = jnp.bfloat16
F32 = jnp.float32


def chunk_count(width):
    for n in (6, 4, 3, 2):
        if width % (16 * n) == 0:
            return n
    return 1


def dot(a, b, dims):
    return lax.dot_general(a, b, dims, preferred_element_type=F32)


def kernel(
    ctx_n,
    pipe_n,
    reach,
    up_h,
    xin_h,
    inv_h,
    gain_h,
    q_h,
    k_h,
    v_h,
    ao_h,
    wq_h,
    wk_h,
    wv_h,
    wo_h,
    len_h,
    out_h,
    gath,
    xin,
    inv,
    gain,
    q,
    kb,
    vb,
    ao,
    wq,
    wk,
    wv,
    wo,
    slen,
    wo_cut,
    gain_col,
    ao_t,
    q_t,
    k_t,
    do_t,
    s,
    part_k,
    part_v,
    snd_k,
    snd_v,
    rcv_k,
    rcv_v,
    dq,
    pacc,
    rs_a,
    rs_ar,
    rs_b,
    rs_br,
    rs_c,
    rs_cr,
    res,
    lsem,
    k_s,
    k_r,
    v_s,
    v_r,
    ag_s,
    ag_r,
    dk_s,
    dk_r,
    dv_s,
    dv_r,
    rs_s,
    rs_rv,
    x_s,
    x_r,
):
    i = lax.axis_index("ctx")
    p = lax.axis_index("pipe")
    t = lax.axis_index("tp")
    partner = t + 1 - 2 * (t % 2)
    cross = (t + 2) % 4
    diag = 3 - t
    rows = q.shape[0]
    width = xin.shape[0]
    kv_heads = kb.shape[2] // HEAD_SIZE
    group = q.shape[1] // kb.shape[2]
    stacked = group * rows
    scale = QUERY_SCALAR ** (-0.5)
    model_width = width * 4
    chunks = chunk_count(width)
    chunk = width // chunks

    def local(src, dst, n):
        c = pltpu.make_async_copy(src, dst, lsem.at[n])
        c.start()
        return c

    def remote(src, dst, ss, rs, dev):
        return pltpu.make_async_remote_copy(
            src_ref=src,
            dst_ref=dst,
            send_sem=ss,
            recv_sem=rs,
            device_id=dev,
            device_id_type=pl.DeviceIdType.MESH,
        )

    barrier = pltpu.get_barrier_semaphore()

    def greet(dev):
        pl.semaphore_signal(
            barrier, inc=1, device_id=dev, device_id_type=pl.DeviceIdType.MESH
        )

    has_up = i + 1 < ctx_n
    has_down = i > 0

    @pl.when(has_up)
    def _():
        greet({"ctx": i + 1})

    @pl.when(has_down)
    def _():
        greet({"ctx": i - 1})

    greet({"tp": partner})
    greet({"tp": cross})
    expect = 2
    prev = (p + pipe_n - 1) % pipe_n
    if pipe_n > 1:
        greet({"pipe": prev})
        expect += 1
    if pipe_n > 2:
        greet({"pipe": (p + 1) % pipe_n})
        expect += 1

    c_k = local(k_h, kb.at[0], 0)
    c_q = local(q_h, q, 1)
    c_len = local(len_h, slen, 2)
    c_up = local(up_h, gath.at[t], 3)
    c_wo = local(wo_h, wo, 5)
    c_ao = local(ao_h, ao, 6)
    c_gain = local(gain_h, gain, 12)
    c_v = local(v_h, vb.at[0], 4)
    c_wq = local(wq_h, wq, 7)
    c_wk = local(wk_h, wk, 8)
    c_wv = local(wv_h, wv, 9)
    c_xin = local(xin_h, xin, 10)
    c_inv = local(inv_h, inv, 11)

    pl.semaphore_wait(
        barrier, expect + jnp.where(has_up, 1, 0) + jnp.where(has_down, 1, 0)
    )

    up_dev = {"ctx": i + 1}
    down_dev = {"ctx": i - 1}

    def k_copy(d):
        src = k_h if d == 0 else kb.at[d]
        return remote(src, kb.at[d + 1], k_s.at[d], k_r.at[d + 1], up_dev)

    def v_copy(d):
        src = v_h if d == 0 else vb.at[d]
        return remote(src, vb.at[d + 1], v_s.at[d], v_r.at[d + 1], up_dev)

    half = width // GATHER_PARTS

    def ag_cross(n):
        sl = pl.ds(n * half, half)
        return remote(up_h.at[sl], gath.at[t, sl], ag_s.at[n], ag_r.at[n], {"tp": cross})

    def ag_fwd(n):
        sl = pl.ds(n * half, half)
        m = GATHER_PARTS + n
        return remote(
            gath.at[cross, sl], gath.at[cross, sl], ag_s.at[m], ag_r.at[m], {"tp": partner}
        )

    own_slot = 2 * GATHER_PARTS
    ag_part = remote(
        up_h, gath.at[t], ag_s.at[own_slot], ag_r.at[own_slot], {"tp": partner}
    )
    for n in range(GATHER_PARTS):
        ag_cross(n).start()

    @pl.when(has_up)
    def _():
        k_copy(0).start()
        v_copy(0).start()

    ag_part.start()

    c_len.wait()
    length = slen[0]
    key_i = lax.broadcasted_iota(jnp.int32, (rows, stacked), 0)
    qry_i = lax.broadcasted_iota(jnp.int32, (rows, stacked), 1) % rows
    later0 = qry_i - key_i
    pos_q = i * rows + qry_i
    live = pos_q < length

    def head_cols(h):
        return slice(h * HEAD_SIZE, (h + 1) * HEAD_SIZE)

    def flip(x):
        return x.astype(F32).T

    def scores(d):
        later = later0 + d * rows
        pos_k = pos_q - later
        ok = (later >= 0) & (later < WINDOW) & (pos_k < length) & live
        for g in range(kv_heads):
            keys = kb[d, :, head_cols(g)]
            sc = dot(keys, q_t[g], NN) * scale
            s[d, g] = jnp.where(ok, sc, NEG_FILL)
            k_t[d, g] = flip(keys).astype(BF)

    c_q.wait()
    for g in range(kv_heads):
        for r in range(group):
            q_t[g, :, r * rows : (r + 1) * rows] = flip(q[:, head_cols(g * group + r)]).astype(BF)
    c_k.wait()
    scores(0)
    c_ao.wait()
    for h in range(kv_heads * group):
        ao_t[head_cols(h), :] = flip(ao[:, head_cols(h)])
    c_wo.wait()
    for n in range(4):
        wo_cut[n] = wo[:, n * width : (n + 1) * width]
    c_gain.wait()
    gain_col[...] = jnp.broadcast_to(gain[...], (rows, width)).T

    def take_k(d):
        @pl.when(i >= d)
        def _():
            k_copy(d - 1).wait_recv()
            if d < reach:

                @pl.when(has_up)
                def _():
                    k_copy(d).start()

            scores(d)

    def pass_v(d):
        if d < reach:

            @pl.when(has_up & (i >= d))
            def _():
                v_copy(d - 1).wait_recv()
                v_copy(d).start()

    def need_v(d):
        if d < reach:

            @pl.when(i + 1 >= ctx_n)
            def _():
                v_copy(d - 1).wait_recv()

        else:
            v_copy(d - 1).wait_recv()

    c_up.wait()
    acc = dot(wo_cut[t], gath[t], NN)
    if reach >= 1:
        take_k(1)
    ag_cross(0).wait_recv()
    ag_fwd(0).start()
    if reach >= 1:
        pass_v(1)
    for n in range(1, GATHER_PARTS):
        ag_cross(n).wait_recv()
        ag_fwd(n).start()
    for d in range(2, reach + 1):
        take_k(d)
        pass_v(d)
    ag_part.wait_recv()
    acc = acc + dot(wo_cut[partner], gath[partner], NN)
    acc = acc + dot(wo_cut[cross], gath[cross], NN)

    for d in range(1, reach + 1):

        @pl.when(i < d)
        def _():
            s[d] = jnp.full(s.shape[1:], NEG_FILL, F32)

    for g in range(kv_heads):
        top = jnp.max(s[0, g], axis=0, keepdims=True)
        for d in range(1, reach + 1):
            top = jnp.maximum(top, jnp.max(s[d, g], axis=0, keepdims=True))
        total = jnp.zeros((1, stacked), F32)
        for d in range(reach + 1):
            val = s[d, g]
            e = jnp.where(val > 0.5 * NEG_FILL, jnp.exp(val - top), 0.0)
            s[d, g] = e
            total = total + jnp.sum(e, axis=0, keepdims=True)
        inv_total = 1.0 / jnp.where(live[:1], total, 1.0)
        for d in range(reach + 1):
            s[d, g] = s[d, g] * inv_total

    for n in range(GATHER_PARTS):
        ag_fwd(n).wait_recv()
    acc = acc + dot(wo_cut[diag], gath[diag], NN)
    grad = acc.astype(BF)
    deltas = []
    for g in range(kv_heads):
        sums = []
        for r in range(group):
            h = g * group + r
            part = grad[head_cols(h)]
            do_t[g, :, r * rows : (r + 1) * rows] = part
            sums.append(
                jnp.sum(part.astype(F32) * ao_t[head_cols(h), :], axis=0, keepdims=True)
            )
        deltas.append(jnp.concatenate(sums, axis=1))

    def dk_copy(d, g):
        return remote(
            snd_k.at[d, g], rcv_k.at[d - 1, g], dk_s.at[d, g], dk_r.at[d - 1, g], down_dev
        )

    def dv_copy(d, g):
        return remote(
            snd_v.at[d, g], rcv_v.at[d - 1, g], dv_s.at[d, g], dv_r.at[d - 1, g], down_dev
        )

    dq[...] = jnp.zeros_like(dq)

    def first_of_chain(d):
        return i + 1 >= ctx_n if d < reach else i >= d

    def block(d):
        for g in range(kv_heads):
            part_v[d, g] = dot(s[d, g].astype(BF), do_t[g], NT)
            if d > 0:

                @pl.when(first_of_chain(d))
                def _():
                    snd_v[d, g] = part_v[d, g].astype(BF)
                    dv_copy(d, g).start()

        if d > 0:
            need_v(d)
        for g in range(kv_heads):
            dprob = dot(vb[d, :, head_cols(g)], do_t[g], NN)
            ds = (s[d, g] * (dprob - deltas[g])).astype(BF)
            part_k[d, g] = dot(ds, q_t[g], NT)
            if d > 0:

                @pl.when(first_of_chain(d))
                def _():
                    snd_k[d, g] = part_k[d, g].astype(BF)
                    dk_copy(d, g).start()

            dq[g] += dot(k_t[d, g], ds, NN)

    for d in range(reach, 0, -1):
        pl.when(i >= d)(functools.partial(block, d))
    c_v.wait()
    block(0)

    coupling = jnp.zeros((1, rows), F32)
    low = []
    for g in range(kv_heads):
        for r in range(group):
            cols = slice(r * rows, (r + 1) * rows)
            part = (dq[g, :, cols] * scale).astype(BF)
            low.append(part)
            coupling = coupling + jnp.sum(
                part.astype(F32) * q_t[g, :, cols].astype(F32), axis=0, keepdims=True
            )
    dq_low = jnp.concatenate(low, axis=0)
    owners = (diag, cross, partner, t)

    def piece_rows(n):
        return pl.ds(pl.multiple_of(owners[n] * width, 16), width)

    def query_piece(n):
        pacc[n] = dot(wq[piece_rows(n), :], dq_low, NN)

    c_wq.wait()
    done = 0
    for d in range(reach - 1, 0, -1):

        @pl.when(has_up & (i >= d))
        def _():
            for g in range(kv_heads):
                dv_copy(d + 1, g).wait_recv()
                snd_v[d, g] = (part_v[d, g] + rcv_v[d, g].astype(F32)).astype(BF)
                dv_copy(d, g).start()
            for g in range(kv_heads):
                dk_copy(d + 1, g).wait_recv()
                snd_k[d, g] = (part_k[d, g] + rcv_k[d, g].astype(F32)).astype(BF)
                dk_copy(d, g).start()

        if done < 4:
            query_piece(done)
            done += 1
    while done < 4:
        query_piece(done)
        done += 1
    c_wk.wait()
    c_wv.wait()
    c_xin.wait()
    c_inv.wait()
    if reach >= 1:

        @pl.when(has_up)
        def _():
            for g in range(kv_heads):
                dv_copy(1, g).wait_recv()
                part_v[0, g] += rcv_v[0, g].astype(F32)

    dv_low = jnp.concatenate([part_v[0, g].astype(BF) for g in range(kv_heads)], axis=1)
    for n in range(4):
        pacc[n] += dot(wv[piece_rows(n), :], dv_low, NT)
    if reach >= 1:

        @pl.when(has_up)
        def _():
            for g in range(kv_heads):
                dk_copy(1, g).wait_recv()
                part_k[0, g] += rcv_k[0, g].astype(F32)

    dk_low = jnp.concatenate(
        [(part_k[0, g] * scale).astype(BF) for g in range(kv_heads)], axis=1
    )
    both = dk_low.astype(F32) * kb[0].astype(F32) + dv_low.astype(F32) * vb[0].astype(F32)
    for g in range(kv_heads):
        coupling = coupling + jnp.sum(both[:, head_cols(g)].T, axis=0, keepdims=True)

    def piece(n):
        return pacc[n] + dot(wk[piece_rows(n), :], dk_low, NT)

    lead = COUPLING_ROWS
    wide = jnp.broadcast_to(coupling, (lead, rows))

    send_a = remote(rs_a, rs_ar, rs_s.at[0], rs_rv.at[0], {"tp": partner})
    send_c = remote(rs_c, rs_cr, rs_s.at[1], rs_rv.at[1], {"tp": partner})

    def b_copy(n):
        sl = pl.ds(0, lead + chunk) if n == 0 else pl.ds(lead + n * chunk, chunk)
        return remote(
            rs_b.at[sl], rs_br.at[sl], rs_s.at[2 + n], rs_rv.at[2 + n], {"tp": cross}
        )

    def x_copy(n):
        sl = pl.ds(n * chunk, chunk)
        if pipe_n == 1:
            return pltpu.make_async_copy(res.at[sl], out_h.at[sl], x_s.at[n])
        return remote(res.at[sl], out_h.at[sl], x_s.at[n], x_r.at[n], {"pipe": prev})

    rs_a[lead:, :] = piece(0).astype(BF)
    rs_a[:lead, :] = wide.astype(BF)
    send_a.start()
    pacc[1] = piece(1)
    send_a.wait_recv()
    rs_b[:lead, :] = (wide + rs_ar[:lead, :].astype(F32)).astype(BF)
    for n in range(chunks):
        sl = slice(n * chunk, (n + 1) * chunk)
        sh = slice(lead + n * chunk, lead + (n + 1) * chunk)
        rs_b[sh, :] = (pacc[1, sl] + rs_ar[sh, :].astype(F32)).astype(BF)
        b_copy(n).start()
    rs_c[lead:, :] = piece(2).astype(BF)
    rs_c[:lead, :] = wide.astype(BF)
    send_c.start()
    pacc[3] = piece(3)
    iv = inv[...]
    send_c.wait_recv()
    for n in range(chunks):
        sl = slice(n * chunk, (n + 1) * chunk)
        sh = slice(lead + n * chunk, lead + (n + 1) * chunk)
        b_copy(n).wait_recv()
        if n == 0:
            coup = (
                coupling + rs_cr[:lead, :].astype(F32)[:1] + rs_br[:lead, :].astype(F32)[:1]
            )
            drag = iv * coup / model_width
        normed = pacc[3, sl] + rs_cr[sh, :].astype(F32) + rs_br[sh, :].astype(F32)
        val = gath[t, sl, :].astype(F32) + iv * (
            gain_col[sl, :] * normed - xin[sl, :].astype(F32) * drag
        )
        res[sl, :] = val.astype(BF)
        x_copy(n).start()

    for n in range(GATHER_PARTS):
        ag_cross(n).wait_send()
        ag_fwd(n).wait_send()
    ag_part.wait_send()
    for d in range(reach):

        @pl.when(has_up & (i >= d))
        def _():
            k_copy(d).wait_send()
            v_copy(d).wait_send()

    for d in range(1, reach + 1):

        @pl.when(i >= d)
        def _():
            for g in range(kv_heads):
                dv_copy(d, g).wait_send()
                dk_copy(d, g).wait_send()

    send_a.wait_send()
    send_c.wait_send()
    for n in range(chunks):
        b_copy(n).wait_send()
    for n in range(chunks):
        x_copy(n).wait()


def per_device(up, xin, inv, gain, q, k, v, ao, wq, wk, wv, wo, lens):
    ctx_n = lax.axis_size("ctx")
    pipe_n = lax.axis_size("pipe")
    tp_n = lax.axis_size("tp")
    assert tp_n == 4
    up, xin, q, k, v, ao = up[0].T, xin[0].T, q[0], k[0], v[0], ao[0]
    wq, wk, wv, wo = wq[0], wk[0], wv[0], wo[0]
    width, rows = up.shape
    reach = min((WINDOW - 2 + rows) // rows, ctx_n - 1)
    kv_cols, q_cols = k.shape[1], q.shape[1]
    kv_heads = kv_cols // HEAD_SIZE
    stacked = rows * (q_cols // kv_cols)
    chunks = chunk_count(width)
    vm = pltpu.VMEM
    dma = pltpu.SemaphoreType.DMA
    blocks = reach + 1
    scratch = [
        vm((tp_n, width, rows), BF),
        vm((width, rows), BF),
        vm(inv.shape, F32),
        vm(gain.shape, F32),
        vm(q.shape, BF),
        vm((blocks, rows, kv_cols), BF),
        vm((blocks, rows, kv_cols), BF),
        vm(ao.shape, BF),
        vm(wq.shape, BF),
        vm(wk.shape, BF),
        vm(wv.shape, BF),
        vm(wo.shape, BF),
        pltpu.SMEM(lens.shape, jnp.int32),
        vm((tp_n, wo.shape[0], width), BF),
        vm((width, rows), F32),
        vm((q_cols, rows), F32),
        vm((kv_heads, HEAD_SIZE, stacked), BF),
        vm((blocks, kv_heads, HEAD_SIZE, rows), BF),
        vm((kv_heads, HEAD_SIZE, stacked), BF),
        vm((blocks, kv_heads, rows, stacked), F32),
        vm((blocks, kv_heads, rows, HEAD_SIZE), F32),
        vm((blocks, kv_heads, rows, HEAD_SIZE), F32),
        vm((blocks, kv_heads, rows, HEAD_SIZE), BF),
        vm((blocks, kv_heads, rows, HEAD_SIZE), BF),
        vm((blocks, kv_heads, rows, HEAD_SIZE), BF),
        vm((blocks, kv_heads, rows, HEAD_SIZE), BF),
        vm((kv_heads, HEAD_SIZE, stacked), F32),
        vm((tp_n, width, rows), F32),
    ]
    scratch += [vm((COUPLING_ROWS + width, rows), BF)] * 6
    scratch += [vm((width, rows), BF)]
    scratch += [dma((13,))]
    scratch += [dma((blocks,))] * 4
    scratch += [dma((2 * GATHER_PARTS + 1,))] * 2
    scratch += [dma((blocks, kv_heads))] * 4
    scratch += [dma((2 + chunks,))] * 2
    scratch += [dma((chunks,))] * 2
    out = pl.pallas_call(
        functools.partial(kernel, ctx_n, pipe_n, reach),
        out_shape=jax.ShapeDtypeStruct((width, rows), BF),
        in_specs=[pl.BlockSpec(memory_space=pl.ANY)] * 13,
        out_specs=pl.BlockSpec(memory_space=pl.ANY),
        scratch_shapes=scratch,
        compiler_params=pltpu.CompilerParams(collective_id=0, has_side_effects=True),
        name="layer_backward",
    )(up, xin, inv, gain, q, k, v, ao, wq, wk, wv, wo, lens)
    return out.T[None]


def solution(mesh):
    placed = (
        P("pipe", "ctx", "tp"),
        P("pipe", "ctx", "tp"),
        P("pipe", "ctx"),
        P("pipe", "tp"),
        P("pipe", "ctx", "tp"),
        P("pipe", "ctx", "tp"),
        P("pipe", "ctx", "tp"),
        P("pipe", "ctx", "tp"),
        P("pipe", None, "tp"),
        P("pipe", None, "tp"),
        P("pipe", None, "tp"),
        P("pipe", "tp", None),
        P("pipe"),
    )
    return jax.shard_map(
        per_device, mesh=mesh, in_specs=placed, out_specs=P("pipe", "ctx", "tp"), check_vma=False
    )
```

profile of v0, /device:TPU:0, one launch (start us, length us, event | category | flops | bytes accessed | tf_op | source)
XLA Modules:
  0.0 40.8 jit_solution(3240978080324256485)
XLA Ops:
  0.7 38.5 %layer_backward.1 = bf16[672,128]{1,0:T(8,128)(2,1)} custom-call(bf16[672,128]{1,0:T(8,128)(2,1)} %bitcast.22, bf16[672,128]{1,0:T(8,128)(2,1)} %bitcast.23, f32[1,128]{1,0:T(1,128)} %inv_h.1, f32[1,672]{1,0:T(1,128)} %gain_h.1, bf16[128,512]{1,0:T(8,128)(2,1)} %bitcast.24, bf16[128,256]{1,0:T(8,128)(2,1)} %bitcast.26, bf16[128,256]{1,0:T(8,128)(2,1)} %bitcast.27, ...), custom_call_target="tpu_custom_call" | custom-call | tf_op jit(solution)/shard_map/layer_backward/pallas_call | solution.py:594
  39.2 1.6 %copy.16 = bf16[1,128,672]{1,2,0:T(8,128)(2,1)} copy(bf16[1,128,672]{1,2,0:T(8,128)(2,1)} %bitcast.21) | data formatting | bytes 344064
where the time goes:
time: 40.9 us; the launch traced here: 40.8 us
  Pallas kernels  38.5 us (94%)
  local copies, waits for them, and re-layouts  1.6 us (4%)
  between operations  0.66 us (2%)
    pallas_call x1, Pallas kernels, per_device(): pl.pallas_call(functools.partial(kernel, ctx_n, pipe_n, reach), out_shape...  38.5 us
    unnamed x1, local copies, waits for them, and re-layouts  1.6 us

commit v1 on v0

v1 whole, which is shorter than its diff:
```python
import functools

import jax
import jax.numpy as jnp
from jax import lax
from jax.experimental import pallas as pl
from jax.experimental.pallas import tpu as pltpu
from jax.sharding import PartitionSpec as P

QUERY_HEADS = 16
KEY_VALUE_HEADS = 8
HEAD_SIZE = 128
WINDOW = 1024
QUERY_SCALAR = 168
NEG_FILL = -1e30
GATHER_ROWS = 256
COUPLING_ROWS = 16
NT = (((1,), (1,)), ((), ()))
NN = (((1,), (0,)), ((), ()))
TN = (((0,), (0,)), ((), ()))
BF = jnp.bfloat16
F32 = jnp.float32


def chunk_count(width):
    for n in (6, 4, 3, 2):
        if width % (16 * n) == 0:
            return n
    return 1


def gather_cuts(width):
    return [(at, min(GATHER_ROWS, width - at)) for at in range(0, width, GATHER_ROWS)]


def chunk_groups(chunks):
    groups, first, count = [], 0, 1
    while first < chunks:
        count = min(count, chunks - first)
        groups.append((first, count))
        first, count = first + count, count + 1
    return groups


def direct_reach(reach):
    return [d for d in range(1, reach + 1) if d != 2]


def far_reach(reach):
    return [d for d in direct_reach(reach) if reach >= 2]


def dot(a, b, dims):
    return lax.dot_general(a, b, dims, preferred_element_type=F32)


def kernel(
    ctx_n,
    pipe_n,
    reach,
    up_h,
    xin_h,
    inv_h,
    gain_h,
    q_h,
    k_h,
    v_h,
    ao_h,
    wq_h,
    wk_h,
    wv_h,
    wo_h,
    len_h,
    out_h,
    gath,
    xin,
    inv,
    gain,
    q,
    kb,
    vb,
    ao,
    wq,
    wk,
    wv,
    wo,
    slen,
    wo_cut,
    gain_col,
    ao_t,
    q_t,
    k_t,
    do_t,
    stat,
    s,
    dp,
    ds,
    q_far,
    do_far,
    stat_far,
    s_far,
    part_v,
    part_k,
    snd,
    rcv,
    pacc,
    rs_a,
    rs_ar,
    rs_b,
    rs_br,
    rs_c,
    rs_cr,
    res,
    lsem,
    k_s,
    k_r,
    v_s,
    v_r,
    ag_s,
    ag_r,
    q_s,
    q_r,
    do_s,
    do_r,
    st_s,
    st_r,
    acc_s,
    acc_r,
    rs_s,
    rs_rv,
    x_s,
    x_r,
):
    i = lax.axis_index("ctx")
    p = lax.axis_index("pipe")
    t = lax.axis_index("tp")
    partner = t + 1 - 2 * (t % 2)
    cross = (t + 2) % 4
    diag = 3 - t
    rows = q.shape[0]
    width = xin.shape[0]
    kv_heads = kb.shape[1] // HEAD_SIZE
    group = q.shape[1] // kb.shape[1]
    stacked = group * rows
    scale = QUERY_SCALAR ** (-0.5)
    model_width = width * 4
    chunks = chunk_count(width)
    chunk = width // chunks
    cuts = gather_cuts(width)
    direct = direct_reach(reach)
    far = far_reach(reach)

    def local(src, dst, n):
        c = pltpu.make_async_copy(src, dst, lsem.at[n])
        c.start()
        return c

    def remote(src, dst, ss, rs, dev):
        return pltpu.make_async_remote_copy(
            src_ref=src,
            dst_ref=dst,
            send_sem=ss,
            recv_sem=rs,
            device_id=dev,
            device_id_type=pl.DeviceIdType.MESH,
        )

    barrier = pltpu.get_barrier_semaphore()

    def greet(dev):
        pl.semaphore_signal(
            barrier, inc=1, device_id=dev, device_id_type=pl.DeviceIdType.MESH
        )

    has_up = i + 1 < ctx_n
    has_down = i > 0

    greet({"tp": cross})
    greet({"tp": partner})
    expect = 2
    for d in direct:

        @pl.when(i + d < ctx_n)
        def _():
            greet({"ctx": i + d})

        @pl.when(i >= d)
        def _():
            greet({"ctx": i - d})

        expect = expect + jnp.where(i + d < ctx_n, 1, 0) + jnp.where(i >= d, 1, 0)
    prev = (p + pipe_n - 1) % pipe_n
    if pipe_n > 1:
        greet({"pipe": prev})
        expect += 1
    if pipe_n > 2:
        greet({"pipe": (p + 1) % pipe_n})
        expect += 1

    c_q = local(q_h, q, 1)
    c_k = local(k_h, kb.at[pl.ds(0, rows)], 0)
    c_len = local(len_h, slen, 2)
    c_up = local(up_h, gath.at[t], 3)
    c_wo = local(wo_h, wo, 5)
    c_ao = local(ao_h, ao, 6)
    c_gain = local(gain_h, gain, 12)
    c_v = local(v_h, vb.at[pl.ds(0, rows)], 4)
    c_wq = local(wq_h, wq, 7)
    c_wk = local(wk_h, wk, 8)
    c_wv = local(wv_h, wv, 9)
    c_xin = local(xin_h, xin, 10)
    c_inv = local(inv_h, inv, 11)

    def head_cols(h):
        return slice(h * HEAD_SIZE, (h + 1) * HEAD_SIZE)

    def block_rows(d):
        return slice(d * rows, (d + 1) * rows)

    def flip(x):
        return x.astype(F32).T

    c_q.wait()
    for g in range(kv_heads):
        for r in range(group):
            q_t[g, :, block_rows(r)] = flip(q[:, head_cols(g * group + r)]).astype(BF)

    pl.semaphore_wait(barrier, expect)

    def kv_copy(src_h, buf, ss, rs, d):
        dst = buf.at[pl.ds(d * rows, rows)]
        if d == 2:
            return remote(buf.at[pl.ds(rows, rows)], dst, ss.at[d], rs.at[d], {"ctx": i + 1})
        return remote(src_h, dst, ss.at[d], rs.at[d], {"ctx": i + d})

    def k_copy(d):
        return kv_copy(k_h, kb, k_s, k_r, d)

    def v_copy(d):
        return kv_copy(v_h, vb, v_s, v_r, d)

    def sends_up(d):
        return has_up & has_down if d == 2 else i + d < ctx_n

    def q_copy(n):
        return remote(q_t, q_far.at[n], q_s.at[n], q_r.at[n], {"ctx": i - far[n]})

    def do_copy(n, g):
        return remote(
            do_t.at[g], do_far.at[n, g], do_s.at[n, g], do_r.at[n, g], {"ctx": i - far[n]}
        )

    def stat_copy(n):
        return remote(stat, stat_far.at[n], st_s.at[n], st_r.at[n], {"ctx": i - far[n]})

    def sends_far(n):
        return i >= 2 if far[n] == 1 else i >= far[n]

    def takes_far(n):
        return has_up & has_down if far[n] == 1 else i + far[n] < ctx_n

    def acc_copy(g):
        return remote(snd.at[g], rcv.at[g], acc_s.at[g], acc_r.at[g], {"ctx": i - 1})

    parts = len(cuts)

    def ag_cross(n):
        sl = pl.ds(*cuts[n])
        return remote(up_h.at[sl], gath.at[t, sl], ag_s.at[n], ag_r.at[n], {"tp": cross})

    def ag_fwd(n):
        sl = pl.ds(*cuts[n])
        m = parts + n
        return remote(
            gath.at[cross, sl], gath.at[cross, sl], ag_s.at[m], ag_r.at[m], {"tp": partner}
        )

    ag_part = remote(
        up_h, gath.at[t], ag_s.at[2 * parts], ag_r.at[2 * parts], {"tp": partner}
    )
    for n in range(parts):
        ag_cross(n).start()
    for d in direct:

        @pl.when(sends_up(d))
        def _():
            k_copy(d).start()

    for n in range(len(far)):

        @pl.when(sends_far(n))
        def _():
            q_copy(n).start()

    ag_part.start()
    for d in direct:

        @pl.when(sends_up(d))
        def _():
            v_copy(d).start()

    for d in range(1, reach + 1):

        @pl.when(i < d)
        def _():
            kb[block_rows(d)] = jnp.zeros((rows, kb.shape[1]), BF)
            vb[block_rows(d)] = jnp.zeros((rows, vb.shape[1]), BF)

    c_len.wait()
    length = slen[0]
    key_i = lax.broadcasted_iota(jnp.int32, (rows, stacked), 0)
    qry_i = lax.broadcasted_iota(jnp.int32, (rows, stacked), 1) % rows
    later0 = qry_i - key_i
    pos_q = i * rows + qry_i
    live = (pos_q < length)[:1]

    def allowed(query_pos, d):
        later = later0 + d * rows
        pos_k = query_pos - later
        ok = (later >= 0) & (later < WINDOW) & (pos_k < length) & (query_pos < length)
        return ok & (pos_k >= 0)

    def scores(d):
        ok = allowed(pos_q, d)
        for g in range(kv_heads):
            keys = kb[block_rows(d), head_cols(g)]
            sc = dot(keys, q_t[g], NN) * scale
            s[g, block_rows(d)] = jnp.where(ok, sc, NEG_FILL)
            k_t[g, :, block_rows(d)] = flip(keys).astype(BF)

    c_k.wait()
    scores(0)
    c_wo.wait()
    for n in range(4):
        wo_cut[n] = wo[:, n * width : (n + 1) * width]
    c_ao.wait()
    for h in range(kv_heads * group):
        ao_t[head_cols(h), :] = flip(ao[:, head_cols(h)])
    c_gain.wait()
    gain_col[...] = jnp.broadcast_to(gain[...], (rows, width)).T

    c_up.wait()
    acc = dot(wo_cut[t], gath[t], NN)
    ag_part.wait_recv()
    acc = acc + dot(wo_cut[partner], gath[partner], NN)

    def take(copy, d):
        @pl.when(i >= d)
        def _():
            copy(d).wait_recv()

    def pass_on(copy):
        if reach >= 2:

            @pl.when(sends_up(2))
            def _():
                copy(2).start()

    if reach >= 1:
        take(k_copy, 1)
        pass_on(k_copy)
        scores(1)

    for n, (at, size) in enumerate(cuts):
        ag_cross(n).wait_recv()
        ag_fwd(n).start()
        acc = acc + dot(wo_cut[cross, :, at : at + size], gath[cross, at : at + size], NN)
    if reach >= 1:
        take(v_copy, 1)
        pass_on(v_copy)
    for n, (at, size) in enumerate(cuts):
        ag_fwd(n).wait_recv()
        acc = acc + dot(wo_cut[diag, :, at : at + size], gath[diag, at : at + size], NN)
    grad = acc.astype(BF)
    for g in range(kv_heads):
        for r in range(group):
            do_t[g, :, block_rows(r)] = grad[head_cols(g * group + r)]

    def send_dout(n):
        @pl.when(sends_far(n))
        def _():
            for g in range(kv_heads):
                do_copy(n, g).start()

    def send_stat(n):
        @pl.when(sends_far(n))
        def _():
            stat_copy(n).start()

    if far:
        send_dout(0)

    for g in range(kv_heads):
        sums = []
        for r in range(group):
            h = g * group + r
            sums.append(
                jnp.sum(
                    grad[head_cols(h)].astype(F32) * ao_t[head_cols(h), :], axis=0, keepdims=True
                )
            )
        stat[3 * g + 2 : 3 * g + 3, :] = jnp.concatenate(sums, axis=1)

    for d in range(2, reach + 1):
        take(k_copy, d)
        scores(d)

    for g in range(kv_heads):
        top = jnp.max(s[g], axis=0, keepdims=True)
        total = jnp.zeros((1, stacked), F32)
        for d in range(reach + 1):
            e = jnp.exp(s[g, block_rows(d)] - top)
            s[g, block_rows(d)] = e
            total = total + jnp.sum(e, axis=0, keepdims=True)
        inv_total = jnp.where(live, 1.0 / total, 0.0)
        for d in range(reach + 1):
            s[g, block_rows(d)] = s[g, block_rows(d)] * inv_total
        stat[3 * g : 3 * g + 1, :] = top
        stat[3 * g + 1 : 3 * g + 2, :] = inv_total

    if far:
        send_stat(0)
    for n in range(1, len(far)):
        send_dout(n)
        send_stat(n)

    c_v.wait()
    for d in range(2, reach + 1):
        take(v_copy, d)

    own = min(reach, 1) + 1
    for g in range(kv_heads):
        dp[g] = dot(vb[:, head_cols(g)], do_t[g], NN)
        part_v[g] = dot(s[g, : own * rows].astype(BF), do_t[g], NT)
        delta = stat[3 * g + 2 : 3 * g + 3, :]
        for d in range(reach + 1):
            ds[g, block_rows(d)] = (
                s[g, block_rows(d)] * (dp[g, block_rows(d)] - delta)
            ).astype(BF)
        part_k[g] = dot(ds[g, : own * rows], q_t[g], NT)

    def send_acc(g):
        snd[g, :rows] = part_v[g, block_rows(1)].astype(BF)
        snd[g, rows:] = part_k[g, block_rows(1)].astype(BF)
        acc_copy(g).start()

    if reach >= 1:

        @pl.when(has_down & jnp.logical_not(has_up) if reach >= 2 else has_down)
        def _():
            for g in range(kv_heads):
                send_acc(g)

    coupling = jnp.zeros((1, rows), F32)
    low = []
    for g in range(kv_heads):
        dq = dot(k_t[g], ds[g], NN) * scale
        for r in range(group):
            part = dq[:, block_rows(r)].astype(BF)
            low.append(part)
            coupling = coupling + jnp.sum(
                part.astype(F32) * q_t[g, :, block_rows(r)].astype(F32), axis=0, keepdims=True
            )
    dq_low = jnp.concatenate(low, axis=0)
    owners = (diag, cross, partner, t)

    def piece_rows(n, at=0, size=width):
        return pl.ds(pl.multiple_of(owners[n] * width + at, 16), size)

    def far_scores(n):
        e = far[n]
        kd, dist = (1, 2) if e == 1 else (0, e)

        @pl.when(takes_far(n))
        def _():
            q_copy(n).wait_recv()
            ok = allowed((i + e) * rows + qry_i, dist)
            for g in range(kv_heads):
                sc = dot(kb[block_rows(kd), head_cols(g)], q_far[n, g], NN) * scale
                s_far[n, g] = jnp.where(ok, sc, NEG_FILL)

    def far_pair(n):
        e = far[n]
        kd = 1 if e == 1 else 0

        @pl.when(takes_far(n))
        def _():
            stat_copy(n).wait_recv()
            for g in range(kv_heads):
                top = stat_far[n, 3 * g : 3 * g + 1, :]
                inv_total = stat_far[n, 3 * g + 1 : 3 * g + 2, :]
                s_far[n, g] = jnp.exp(s_far[n, g] - top) * inv_total
            for g in range(kv_heads):
                delta = stat_far[n, 3 * g + 2 : 3 * g + 3, :]
                do_copy(n, g).wait_recv()
                part_v[g, block_rows(kd)] += dot(s_far[n, g].astype(BF), do_far[n, g], NT)
                dprob = dot(vb[block_rows(kd), head_cols(g)], do_far[n, g], NN)
                dsc = (s_far[n, g] * (dprob - delta)).astype(BF)
                part_k[g, block_rows(kd)] += dot(dsc, q_far[n, g], NT)
                if e == 1:
                    send_acc(g)

    if far:
        far_scores(0)
    c_wq.wait()
    for n in range(4):
        pacc[n] = dot(wq[piece_rows(n), :], dq_low, NN)
    if far:
        far_pair(0)
    for n in range(1, len(far)):
        far_scores(n)
    for n in range(1, len(far)):
        far_pair(n)
    c_wk.wait()
    c_wv.wait()
    c_xin.wait()
    c_inv.wait()
    if reach >= 1:

        @pl.when(has_up)
        def _():
            for g in range(kv_heads):
                acc_copy(g).wait_recv()
                part_v[g, :rows] += rcv[g, :rows].astype(F32)
                part_k[g, :rows] += rcv[g, rows:].astype(F32)

    dv_low = jnp.concatenate([part_v[g, :rows].astype(BF) for g in range(kv_heads)], axis=1)
    dk_low = jnp.concatenate(
        [(part_k[g, :rows] * scale).astype(BF) for g in range(kv_heads)], axis=1
    )
    both = dk_low.astype(F32) * kb[:rows].astype(F32) + dv_low.astype(F32) * vb[:rows].astype(F32)
    for g in range(kv_heads):
        coupling = coupling + jnp.sum(both[:, head_cols(g)].T, axis=0, keepdims=True)

    def piece(n, at=0, size=width):
        span = piece_rows(n, at, size)
        more = dot(wk[span, :], dk_low, NT) + dot(wv[span, :], dv_low, NT)
        return pacc[n, at : at + size] + more

    lead = COUPLING_ROWS
    wide = jnp.broadcast_to(coupling, (lead, rows))

    def span_of(n, count=1):
        return (0, lead + count * chunk) if n == 0 else (lead + n * chunk, count * chunk)

    groups = chunk_groups(chunks)

    def a_copy(m):
        sl = pl.ds(*span_of(*groups[m]))
        return remote(
            rs_a.at[sl], rs_ar.at[sl], rs_s.at[1 + m], rs_rv.at[1 + m], {"tp": partner}
        )

    send_c = remote(rs_c, rs_cr, rs_s.at[0], rs_rv.at[0], {"tp": partner})
    base = 1 + len(groups)

    def b_copy(n):
        sl = pl.ds(*span_of(n))
        return remote(
            rs_b.at[sl], rs_br.at[sl], rs_s.at[base + n], rs_rv.at[base + n], {"tp": cross}
        )

    def x_copy(n):
        sl = pl.ds(n * chunk, chunk)
        if pipe_n == 1:
            return pltpu.make_async_copy(res.at[sl], out_h.at[sl], x_s.at[n])
        return remote(res.at[sl], out_h.at[sl], x_s.at[n], x_r.at[n], {"pipe": prev})

    rs_a[:lead, :] = wide.astype(BF)
    for m, (first, count) in enumerate(groups):
        at, size = first * chunk, count * chunk
        rs_a[lead + at : lead + at + size, :] = piece(0, at, size).astype(BF)
        a_copy(m).start()
    for m, (first, count) in enumerate(groups):
        at, size = first * chunk, count * chunk
        pacc[1, at : at + size] = piece(1, at, size)
        a_copy(m).wait_recv()
        if m == 0:
            rs_b[:lead, :] = (wide + rs_ar[:lead, :].astype(F32)).astype(BF)
        for n in range(first, first + count):
            sl = slice(n * chunk, (n + 1) * chunk)
            sh = slice(lead + n * chunk, lead + (n + 1) * chunk)
            rs_b[sh, :] = (pacc[1, sl] + rs_ar[sh, :].astype(F32)).astype(BF)
            b_copy(n).start()
    rs_c[lead:, :] = piece(2).astype(BF)
    rs_c[:lead, :] = wide.astype(BF)
    send_c.start()
    pacc[3] = piece(3)
    iv = inv[...]
    send_c.wait_recv()
    for n in range(chunks):
        sl = slice(n * chunk, (n + 1) * chunk)
        sh = slice(lead + n * chunk, lead + (n + 1) * chunk)
        b_copy(n).wait_recv()
        if n == 0:
            coup = (
                coupling + rs_cr[:lead, :].astype(F32)[:1] + rs_br[:lead, :].astype(F32)[:1]
            )
            drag = iv * coup / model_width
        normed = pacc[3, sl] + rs_cr[sh, :].astype(F32) + rs_br[sh, :].astype(F32)
        val = gath[t, sl, :].astype(F32) + iv * (
            gain_col[sl, :] * normed - xin[sl, :].astype(F32) * drag
        )
        res[sl, :] = val.astype(BF)
        x_copy(n).start()

    for n in range(parts):
        ag_cross(n).wait_send()
        ag_fwd(n).wait_send()
    ag_part.wait_send()
    for d in range(1, reach + 1):

        @pl.when(sends_up(d))
        def _():
            k_copy(d).wait_send()
            v_copy(d).wait_send()

    for n in range(len(far)):

        @pl.when(sends_far(n))
        def _():
            q_copy(n).wait_send()
            stat_copy(n).wait_send()
            for g in range(kv_heads):
                do_copy(n, g).wait_send()

    if reach >= 1:

        @pl.when(has_down)
        def _():
            for g in range(kv_heads):
                acc_copy(g).wait_send()

    send_c.wait_send()
    for m in range(len(groups)):
        a_copy(m).wait_send()
    for n in range(chunks):
        b_copy(n).wait_send()
    for n in range(chunks):
        x_copy(n).wait()


def per_device(up, xin, inv, gain, q, k, v, ao, wq, wk, wv, wo, lens):
    ctx_n = lax.axis_size("ctx")
    pipe_n = lax.axis_size("pipe")
    tp_n = lax.axis_size("tp")
    assert tp_n == 4
    up, xin, q, k, v, ao = up[0].T, xin[0].T, q[0], k[0], v[0], ao[0]
    wq, wk, wv, wo = wq[0], wk[0], wv[0], wo[0]
    width, rows = up.shape
    reach = min((WINDOW - 2 + rows) // rows, ctx_n - 1)
    kv_cols, q_cols = k.shape[1], q.shape[1]
    kv_heads = kv_cols // HEAD_SIZE
    stacked = rows * (q_cols // kv_cols)
    chunks = chunk_count(width)
    groups = len(chunk_groups(chunks))
    parts = len(gather_cuts(width))
    vm = pltpu.VMEM
    dma = pltpu.SemaphoreType.DMA
    blocks = reach + 1
    own = min(reach, 1) + 1
    far = max(len(far_reach(reach)), 1)
    stats = -(-3 * kv_heads // 8) * 8
    scratch = [
        vm((tp_n, width, rows), BF),
        vm((width, rows), BF),
        vm(inv.shape, F32),
        vm(gain.shape, F32),
        vm(q.shape, BF),
        vm((blocks * rows, kv_cols), BF),
        vm((blocks * rows, kv_cols), BF),
        vm(ao.shape, BF),
        vm(wq.shape, BF),
        vm(wk.shape, BF),
        vm(wv.shape, BF),
        vm(wo.shape, BF),
        pltpu.SMEM(lens.shape, jnp.int32),
        vm((tp_n, wo.shape[0], width), BF),
        vm((width, rows), F32),
        vm((q_cols, rows), F32),
        vm((kv_heads, HEAD_SIZE, stacked), BF),
        vm((kv_heads, HEAD_SIZE, blocks * rows), BF),
        vm((kv_heads, HEAD_SIZE, stacked), BF),
        vm((stats, stacked), F32),
        vm((kv_heads, blocks * rows, stacked), F32),
        vm((kv_heads, blocks * rows, stacked), F32),
        vm((kv_heads, blocks * rows, stacked), BF),
        vm((far, kv_heads, HEAD_SIZE, stacked), BF),
        vm((far, kv_heads, HEAD_SIZE, stacked), BF),
        vm((far, stats, stacked), F32),
        vm((far, kv_heads, rows, stacked), F32),
        vm((kv_heads, own * rows, HEAD_SIZE), F32),
        vm((kv_heads, own * rows, HEAD_SIZE), F32),
        vm((kv_heads, 2 * rows, HEAD_SIZE), BF),
        vm((kv_heads, 2 * rows, HEAD_SIZE), BF),
        vm((tp_n, width, rows), F32),
    ]
    scratch += [vm((COUPLING_ROWS + width, rows), BF)] * 6
    scratch += [vm((width, rows), BF)]
    scratch += [dma((13,))]
    scratch += [dma((blocks,))] * 4
    scratch += [dma((2 * parts + 1,))] * 2
    scratch += [dma((far,))] * 2
    scratch += [dma((far, kv_heads))] * 2
    scratch += [dma((far,))] * 2
    scratch += [dma((kv_heads,))] * 2
    scratch += [dma((1 + groups + chunks,))] * 2
    scratch += [dma((chunks,))] * 2
    out = pl.pallas_call(
        functools.partial(kernel, ctx_n, pipe_n, reach),
        out_shape=jax.ShapeDtypeStruct((width, rows), BF),
        in_specs=[pl.BlockSpec(memory_space=pl.ANY)] * 13,
        out_specs=pl.BlockSpec(memory_space=pl.ANY),
        scratch_shapes=scratch,
        compiler_params=pltpu.CompilerParams(collective_id=0, has_side_effects=True),
        name="layer_backward",
    )(up, xin, inv, gain, q, k, v, ao, wq, wk, wv, wo, lens)
    return out.T[None]


def solution(mesh):
    placed = (
        P("pipe", "ctx", "tp"),
        P("pipe", "ctx", "tp"),
        P("pipe", "ctx"),
        P("pipe", "tp"),
        P("pipe", "ctx", "tp"),
        P("pipe", "ctx", "tp"),
        P("pipe", "ctx", "tp"),
        P("pipe", "ctx", "tp"),
        P("pipe", None, "tp"),
        P("pipe", None, "tp"),
        P("pipe", None, "tp"),
        P("pipe", "tp", None),
        P("pipe"),
    )
    return jax.shard_map(
        per_device, mesh=mesh, in_specs=placed, out_specs=P("pipe", "ctx", "tp"), check_vma=False
    )
```

time: 40.9 us -> 36.8 us (0.90)
  Pallas kernels: 38.5 us -> 34.4 us
    pallas_call x1, Pallas kernels: 38.5 us -> 34.4 us  [per_device(): pl.pallas_call(functools.partial(kernel, ctx_n, pipe_n, reach), out_shape...]
where the time goes in v1:
time: 36.8 us; the launch traced here: 36.7 us
  Pallas kernels  34.4 us (93%)
  local copies, waits for them, and re-layouts  1.6 us (4%)
  between operations  0.66 us (2%)
    pallas_call x1, Pallas kernels, per_device(): pl.pallas_call(functools.partial(kernel, ctx_n, pipe_n, reach), out_shape...  34.4 us
    unnamed x1, local copies, waits for them, and re-layouts  1.6 us

profile of v1, /device:TPU:0, one launch (start us, length us, event | category | flops | bytes accessed | tf_op | source)
XLA Modules:
  0.0 36.7 jit_solution(15234318587945493400)
XLA Ops:
  0.7 34.4 %layer_backward.1 = bf16[672,128]{1,0:T(8,128)(2,1)} custom-call(bf16[672,128]{1,0:T(8,128)(2,1)} %bitcast.22, bf16[672,128]{1,0:T(8,128)(2,1)} %bitcast.23, f32[1,128]{1,0:T(1,128)} %inv_h.1, f32[1,672]{1,0:T(1,128)} %gain_h.1, bf16[128,512]{1,0:T(8,128)(2,1)} %bitcast.24, bf16[128,256]{1,0:T(8,128)(2,1)} %bitcast.26, bf16[128,256]{1,0:T(8,128)(2,1)} %bitcast.27, ...), custom_call_target="tpu_custom_call" | custom-call | tf_op jit(solution)/shard_map/layer_backward/pallas_call | solution.py:709
  35.1 1.6 %copy.16 = bf16[1,128,672]{1,2,0:T(8,128)(2,1)} copy(bf16[1,128,672]{1,2,0:T(8,128)(2,1)} %bitcast.21) | data formatting | bytes 344064

commit v2 on v1

--- a/solution.py
+++ b/solution.py
@@ -14,6 +14,8 @@
 QUERY_SCALAR = 168
 NEG_FILL = -1e30
 GATHER_ROWS = 256
+CHUNK_ROWS = 128
+CHUNK_TAIL = 64
 COUPLING_ROWS = 16
 NT = (((1,), (1,)), ((), ()))
 NN = (((1,), (0,)), ((), ()))
@@ -22,11 +24,15 @@
 F32 = jnp.float32
 
 
-def chunk_count(width):
-    for n in (6, 4, 3, 2):
-        if width % (16 * n) == 0:
-            return n
-    return 1
+def chunk_cuts(width):
+    cuts, at = [], 0
+    while width - at > CHUNK_ROWS + CHUNK_TAIL // 2:
+        cuts.append((at, CHUNK_ROWS))
+        at += CHUNK_ROWS
+    if width - at > CHUNK_TAIL:
+        cuts.append((at, width - at - CHUNK_TAIL))
+        at = width - CHUNK_TAIL
+    return cuts + [(at, width - at)]
 
 
 def gather_cuts(width):
@@ -101,6 +107,7 @@
     s_far,
     part_v,
     part_k,
+    dq_low,
     snd,
     rcv,
     pacc,
@@ -112,9 +119,8 @@
     rs_cr,
     res,
     lsem,
-    k_s,
+    kv_s,
     k_r,
-    v_s,
     v_r,
     ag_s,
     ag_r,
@@ -126,6 +132,8 @@
     st_r,
     acc_s,
     acc_r,
+    from_low,
+    from_high,
     rs_s,
     rs_rv,
     x_s,
@@ -144,8 +152,8 @@
     stacked = group * rows
     scale = QUERY_SCALAR ** (-0.5)
     model_width = width * 4
-    chunks = chunk_count(width)
-    chunk = width // chunks
+    chunk = chunk_cuts(width)
+    chunks = len(chunk)
     cuts = gather_cuts(width)
     direct = direct_reach(reach)
     far = far_reach(reach)
@@ -178,17 +186,17 @@
     greet({"tp": cross})
     greet({"tp": partner})
     expect = 2
-    for d in direct:
-
-        @pl.when(i + d < ctx_n)
-        def _():
-            greet({"ctx": i + d})
-
-        @pl.when(i >= d)
-        def _():
-            greet({"ctx": i - d})
-
-        expect = expect + jnp.where(i + d < ctx_n, 1, 0) + jnp.where(i >= d, 1, 0)
+    if reach >= 1:
+
+        @pl.when(has_down)
+        def _():
+            greet({"ctx": i - 1})
+
+        @pl.when(has_up)
+        def _():
+            greet({"ctx": i + 1})
+
+        expect = expect + jnp.where(has_up, 1, 0) + jnp.where(has_down, 1, 0)
     prev = (p + pipe_n - 1) % pipe_n
     if pipe_n > 1:
         greet({"pipe": prev})
@@ -220,84 +228,111 @@
     def flip(x):
         return x.astype(F32).T
 
+    pl.semaphore_wait(barrier, expect)
+
+    def kv_copy(src_h, buf, ss, rs, d):
+        dst = buf.at[pl.ds(d * rows, rows)]
+        if d == 2:
+            return remote(buf.at[pl.ds(rows, rows)], dst, ss.at[d - 1], rs.at[d - 1], {"ctx": i + 1})
+        return remote(src_h, dst, ss.at[d - 1], rs.at[d - 1], {"ctx": i + d})
+
+    def k_copy(d):
+        return kv_copy(k_h, kb, kv_s, k_r, d)
+
+    def v_copy(d):
+        return kv_copy(v_h, vb, kv_s, v_r, d)
+
+    def sends_up(d):
+        return has_up & has_down if d == 2 else i + d < ctx_n
+
+    def q_copy(n):
+        return remote(q_t, q_far.at[n], q_s.at[n], q_r.at[n], {"ctx": i - far[n]})
+
+    def do_copy(n, g):
+        return remote(
+            do_t.at[g], do_far.at[n, g], do_s.at[n], do_r.at[n, g], {"ctx": i - far[n]}
+        )
+
+    def stat_copy(n):
+        return remote(stat, stat_far.at[n], st_s.at[n], st_r.at[n], {"ctx": i - far[n]})
+
+    def sends_far(n):
+        return i >= 2 if far[n] == 1 else i >= far[n]
+
+    def takes_far(n):
+        return has_up & has_down if far[n] == 1 else i + far[n] < ctx_n
+
+    if reach >= 2:
+        sends_acc = has_down & has_up
+        takes_acc = i + 2 < ctx_n
+    else:
+        sends_acc = has_down
+        takes_acc = has_up
+
+    def acc_copy(g):
+        return remote(snd.at[g], rcv.at[g], acc_s, acc_r.at[g], {"ctx": i - 1})
+
+    parts = len(cuts)
+
+    def ag_cross(n):
+        sl = pl.ds(*cuts[n])
+        return remote(up_h.at[sl], gath.at[t, sl], ag_s, ag_r.at[n], {"tp": cross})
+
+    def ag_fwd(n):
+        sl = pl.ds(*cuts[n])
+        m = parts + n
+        return remote(
+            gath.at[cross, sl], gath.at[cross, sl], ag_s, ag_r.at[m], {"tp": partner}
+        )
+
+    ag_part = remote(
+        up_h, gath.at[t], ag_s, ag_r.at[2 * parts], {"tp": partner}
+    )
+    def token(sem, cond, dev):
+        @pl.when(cond)
+        def _():
+            pl.semaphore_signal(
+                sem, inc=1, device_id=dev, device_id_type=pl.DeviceIdType.MESH
+            )
+
+    def relay(step):
+        if step > 0:
+
+            @pl.when(i >= step + 1)
+            def _():
+                pl.semaphore_wait(from_low, 1)
+
+            @pl.when(i + step + 1 < ctx_n)
+            def _():
+                pl.semaphore_wait(from_high, 1)
+
+        if step + 1 < reach:
+            token(from_low, has_up & (i >= step + 1), {"ctx": i + 1})
+            token(from_high, has_down & (i + step + 1 < ctx_n), {"ctx": i - 1})
+
+    if reach >= 3:
+        relay(0)
+    for n in range(parts):
+        ag_cross(n).start()
+    if reach >= 1:
+
+        @pl.when(has_up)
+        def _():
+            k_copy(1).start()
+            v_copy(1).start()
+
+    ag_part.start()
     c_q.wait()
     for g in range(kv_heads):
         for r in range(group):
             q_t[g, :, block_rows(r)] = flip(q[:, head_cols(g * group + r)]).astype(BF)
 
-    pl.semaphore_wait(barrier, expect)
-
-    def kv_copy(src_h, buf, ss, rs, d):
-        dst = buf.at[pl.ds(d * rows, rows)]
-        if d == 2:
-            return remote(buf.at[pl.ds(rows, rows)], dst, ss.at[d], rs.at[d], {"ctx": i + 1})
-        return remote(src_h, dst, ss.at[d], rs.at[d], {"ctx": i + d})
-
-    def k_copy(d):
-        return kv_copy(k_h, kb, k_s, k_r, d)
-
-    def v_copy(d):
-        return kv_copy(v_h, vb, v_s, v_r, d)
-
-    def sends_up(d):
-        return has_up & has_down if d == 2 else i + d < ctx_n
-
-    def q_copy(n):
-        return remote(q_t, q_far.at[n], q_s.at[n], q_r.at[n], {"ctx": i - far[n]})
-
-    def do_copy(n, g):
-        return remote(
-            do_t.at[g], do_far.at[n, g], do_s.at[n, g], do_r.at[n, g], {"ctx": i - far[n]}
-        )
-
-    def stat_copy(n):
-        return remote(stat, stat_far.at[n], st_s.at[n], st_r.at[n], {"ctx": i - far[n]})
-
-    def sends_far(n):
-        return i >= 2 if far[n] == 1 else i >= far[n]
-
-    def takes_far(n):
-        return has_up & has_down if far[n] == 1 else i + far[n] < ctx_n
-
-    def acc_copy(g):
-        return remote(snd.at[g], rcv.at[g], acc_s.at[g], acc_r.at[g], {"ctx": i - 1})
-
-    parts = len(cuts)
-
-    def ag_cross(n):
-        sl = pl.ds(*cuts[n])
-        return remote(up_h.at[sl], gath.at[t, sl], ag_s.at[n], ag_r.at[n], {"tp": cross})
-
-    def ag_fwd(n):
-        sl = pl.ds(*cuts[n])
-        m = parts + n
-        return remote(
-            gath.at[cross, sl], gath.at[cross, sl], ag_s.at[m], ag_r.at[m], {"tp": partner}
-        )
-
-    ag_part = remote(
-        up_h, gath.at[t], ag_s.at[2 * parts], ag_r.at[2 * parts], {"tp": partner}
-    )
-    for n in range(parts):
-        ag_cross(n).start()
-    for d in direct:
-
-        @pl.when(sends_up(d))
-        def _():
-            k_copy(d).start()
-
-    for n in range(len(far)):
-
-        @pl.when(sends_far(n))
-        def _():
-            q_copy(n).start()
-
-    ag_part.start()
-    for d in direct:
-
-        @pl.when(sends_up(d))
-        def _():
-            v_copy(d).start()
+    if far:
+
+        @pl.when(sends_far(0))
+        def _():
+            q_copy(0).start()
+
 
     for d in range(1, reach + 1):
 
@@ -338,12 +373,28 @@
         ao_t[head_cols(h), :] = flip(ao[:, head_cols(h)])
     c_gain.wait()
     gain_col[...] = jnp.broadcast_to(gain[...], (rows, width)).T
+    if reach >= 3:
+        relay(1)
 
     c_up.wait()
     acc = dot(wo_cut[t], gath[t], NN)
     ag_part.wait_recv()
     acc = acc + dot(wo_cut[partner], gath[partner], NN)
 
+    for step in range(2, reach):
+        relay(step)
+    for d in direct[1:]:
+
+        @pl.when(sends_up(d))
+        def _():
+            k_copy(d).start()
+
+    for n in range(1, len(far)):
+
+        @pl.when(sends_far(n))
+        def _():
+            q_copy(n).start()
+
     def take(copy, d):
         @pl.when(i >= d)
         def _():
@@ -361,25 +412,31 @@
         pass_on(k_copy)
         scores(1)
 
-    for n, (at, size) in enumerate(cuts):
+    def shard_dot(owner, n):
+        at, size = cuts[n]
+        return dot(wo_cut[owner, :, at : at + size], gath[owner, at : at + size], NN)
+
+    for n in range(parts):
         ag_cross(n).wait_recv()
         ag_fwd(n).start()
-        acc = acc + dot(wo_cut[cross, :, at : at + size], gath[cross, at : at + size], NN)
+        acc = acc + shard_dot(cross, n)
+        if n > 0:
+            ag_fwd(n - 1).wait_recv()
+            acc = acc + shard_dot(diag, n - 1)
     if reach >= 1:
         take(v_copy, 1)
         pass_on(v_copy)
-    for n, (at, size) in enumerate(cuts):
-        ag_fwd(n).wait_recv()
-        acc = acc + dot(wo_cut[diag, :, at : at + size], gath[diag, at : at + size], NN)
+    ag_fwd(parts - 1).wait_recv()
+    acc = acc + shard_dot(diag, parts - 1)
     grad = acc.astype(BF)
     for g in range(kv_heads):
         for r in range(group):
             do_t[g, :, block_rows(r)] = grad[head_cols(g * group + r)]
 
-    def send_dout(n):
+    def send_dout(n, heads):
         @pl.when(sends_far(n))
         def _():
-            for g in range(kv_heads):
+            for g in heads:
                 do_copy(n, g).start()
 
     def send_stat(n):
@@ -388,7 +445,7 @@
             stat_copy(n).start()
 
     if far:
-        send_dout(0)
+        send_dout(0, range(1))
 
     for g in range(kv_heads):
         sums = []
@@ -420,9 +477,16 @@
 
     if far:
         send_stat(0)
-    for n in range(1, len(far)):
-        send_dout(n)
-        send_stat(n)
+        for n in range(1, len(far)):
+            send_dout(n, range(1))
+            send_stat(n)
+        for n in range(len(far)):
+            send_dout(n, range(1, kv_heads))
+    for d in direct[1:]:
+
+        @pl.when(sends_up(d))
+        def _():
+            v_copy(d).start()
 
     c_v.wait()
     for d in range(2, reach + 1):
@@ -444,12 +508,19 @@
         snd[g, rows:] = part_k[g, block_rows(1)].astype(BF)
         acc_copy(g).start()
 
-    if reach >= 1:
-
-        @pl.when(has_down & jnp.logical_not(has_up) if reach >= 2 else has_down)
+    if reach == 1:
+
+        @pl.when(has_down)
         def _():
             for g in range(kv_heads):
                 send_acc(g)
+
+    if reach >= 2:
+
+        @pl.when(i != 1)
+        def _():
+            part_v[:, block_rows(1)] = jnp.zeros((kv_heads, rows, HEAD_SIZE), F32)
+            part_k[:, block_rows(1)] = jnp.zeros((kv_heads, rows, HEAD_SIZE), F32)
 
     coupling = jnp.zeros((1, rows), F32)
     low = []
@@ -461,52 +532,61 @@
             coupling = coupling + jnp.sum(
                 part.astype(F32) * q_t[g, :, block_rows(r)].astype(F32), axis=0, keepdims=True
             )
-    dq_low = jnp.concatenate(low, axis=0)
+    dq_low[...] = jnp.concatenate(low, axis=0)
     owners = (diag, cross, partner, t)
 
     def piece_rows(n, at=0, size=width):
         return pl.ds(pl.multiple_of(owners[n] * width + at, 16), size)
 
+    def far_blocks(n):
+        return ((1, 2), (0, 1)) if far[n] == 1 else ((0, far[n]),)
+
     def far_scores(n):
-        e = far[n]
-        kd, dist = (1, 2) if e == 1 else (0, e)
-
         @pl.when(takes_far(n))
         def _():
             q_copy(n).wait_recv()
-            ok = allowed((i + e) * rows + qry_i, dist)
-            for g in range(kv_heads):
-                sc = dot(kb[block_rows(kd), head_cols(g)], q_far[n, g], NN) * scale
-                s_far[n, g] = jnp.where(ok, sc, NEG_FILL)
+            for at, (kd, dist) in enumerate(far_blocks(n)):
+                ok = allowed((i + far[n]) * rows + qry_i, dist)
+                for g in range(kv_heads):
+                    sc = dot(kb[block_rows(kd), head_cols(g)], q_far[n, g], NN) * scale
+                    s_far[n, g, block_rows(at)] = jnp.where(ok, sc, NEG_FILL)
 
     def far_pair(n):
-        e = far[n]
-        kd = 1 if e == 1 else 0
-
         @pl.when(takes_far(n))
         def _():
             stat_copy(n).wait_recv()
-            for g in range(kv_heads):
-                top = stat_far[n, 3 * g : 3 * g + 1, :]
-                inv_total = stat_far[n, 3 * g + 1 : 3 * g + 2, :]
-                s_far[n, g] = jnp.exp(s_far[n, g] - top) * inv_total
+            for at in range(len(far_blocks(n))):
+                for g in range(kv_heads):
+                    top = stat_far[n, 3 * g : 3 * g + 1, :]
+                    inv_total = stat_far[n, 3 * g + 1 : 3 * g + 2, :]
+                    s_far[n, g, block_rows(at)] = (
+                        jnp.exp(s_far[n, g, block_rows(at)] - top) * inv_total
+                    )
             for g in range(kv_heads):
                 delta = stat_far[n, 3 * g + 2 : 3 * g + 3, :]
                 do_copy(n, g).wait_recv()
-                part_v[g, block_rows(kd)] += dot(s_far[n, g].astype(BF), do_far[n, g], NT)
-                dprob = dot(vb[block_rows(kd), head_cols(g)], do_far[n, g], NN)
-                dsc = (s_far[n, g] * (dprob - delta)).astype(BF)
-                part_k[g, block_rows(kd)] += dot(dsc, q_far[n, g], NT)
-                if e == 1:
-                    send_acc(g)
+                for at, (kd, _) in enumerate(far_blocks(n)):
+                    pr = s_far[n, g, block_rows(at)]
+                    part_v[g, block_rows(kd)] += dot(pr.astype(BF), do_far[n, g], NT)
+                    dprob = dot(vb[block_rows(kd), head_cols(g)], do_far[n, g], NN)
+                    dsc = (pr * (dprob - delta)).astype(BF)
+                    part_k[g, block_rows(kd)] += dot(dsc, q_far[n, g], NT)
+                    if kd == 1:
+                        send_acc(g)
+
+    def project_query():
+        c_wq.wait()
+        for n in range(4):
+            pacc[n] = dot(wq[piece_rows(n), :], dq_low[...], NN)
 
     if far:
+        early = i < 2
         far_scores(0)
-    c_wq.wait()
-    for n in range(4):
-        pacc[n] = dot(wq[piece_rows(n), :], dq_low, NN)
-    if far:
+        pl.when(early)(project_query)
         far_pair(0)
+        pl.when(jnp.logical_not(early))(project_query)
+    else:
+        project_query()
     for n in range(1, len(far)):
         far_scores(n)
     for n in range(1, len(far)):
@@ -517,7 +597,7 @@
     c_inv.wait()
     if reach >= 1:
 
-        @pl.when(has_up)
+        @pl.when(takes_acc)
         def _():
             for g in range(kv_heads):
                 acc_copy(g).wait_recv()
@@ -540,46 +620,44 @@
     lead = COUPLING_ROWS
     wide = jnp.broadcast_to(coupling, (lead, rows))
 
-    def span_of(n, count=1):
-        return (0, lead + count * chunk) if n == 0 else (lead + n * chunk, count * chunk)
+    def span_of(first, count=1):
+        at, size = chunk[first][0], sum(chunk[n][1] for n in range(first, first + count))
+        return (0, lead + size) if first == 0 else (lead + at, size)
 
     groups = chunk_groups(chunks)
 
     def a_copy(m):
         sl = pl.ds(*span_of(*groups[m]))
-        return remote(
-            rs_a.at[sl], rs_ar.at[sl], rs_s.at[1 + m], rs_rv.at[1 + m], {"tp": partner}
-        )
-
-    send_c = remote(rs_c, rs_cr, rs_s.at[0], rs_rv.at[0], {"tp": partner})
+        return remote(rs_a.at[sl], rs_ar.at[sl], rs_s.at[0], rs_rv.at[1 + m], {"tp": partner})
+
+    send_c = remote(rs_c, rs_cr, rs_s.at[1], rs_rv.at[0], {"tp": partner})
     base = 1 + len(groups)
 
     def b_copy(n):
         sl = pl.ds(*span_of(n))
-        return remote(
-            rs_b.at[sl], rs_br.at[sl], rs_s.at[base + n], rs_rv.at[base + n], {"tp": cross}
-        )
-
-    def x_copy(n):
-        sl = pl.ds(n * chunk, chunk)
+        return remote(rs_b.at[sl], rs_br.at[sl], rs_s.at[2], rs_rv.at[base + n], {"tp": cross})
+
+    def x_copy(at, size):
+        sl = pl.ds(at, size)
         if pipe_n == 1:
-            return pltpu.make_async_copy(res.at[sl], out_h.at[sl], x_s.at[n])
-        return remote(res.at[sl], out_h.at[sl], x_s.at[n], x_r.at[n], {"pipe": prev})
+            return pltpu.make_async_copy(res.at[sl], out_h.at[sl], x_s)
+        return remote(res.at[sl], out_h.at[sl], x_s, x_r, {"pipe": prev})
 
     rs_a[:lead, :] = wide.astype(BF)
     for m, (first, count) in enumerate(groups):
-        at, size = first * chunk, count * chunk
+        at, size = chunk[first][0], sum(chunk[n][1] for n in range(first, first + count))
         rs_a[lead + at : lead + at + size, :] = piece(0, at, size).astype(BF)
         a_copy(m).start()
     for m, (first, count) in enumerate(groups):
-        at, size = first * chunk, count * chunk
+        at, size = chunk[first][0], sum(chunk[n][1] for n in range(first, first + count))
         pacc[1, at : at + size] = piece(1, at, size)
         a_copy(m).wait_recv()
         if m == 0:
             rs_b[:lead, :] = (wide + rs_ar[:lead, :].astype(F32)).astype(BF)
         for n in range(first, first + count):
-            sl = slice(n * chunk, (n + 1) * chunk)
-            sh = slice(lead + n * chunk, lead + (n + 1) * chunk)
+            at, size = chunk[n]
+            sl = slice(at, at + size)
+            sh = slice(lead + at, lead + at + size)
             rs_b[sh, :] = (pacc[1, sl] + rs_ar[sh, :].astype(F32)).astype(BF)
             b_copy(n).start()
     rs_c[lead:, :] = piece(2).astype(BF)
@@ -589,8 +667,9 @@
     iv = inv[...]
     send_c.wait_recv()
     for n in range(chunks):
-        sl = slice(n * chunk, (n + 1) * chunk)
-        sh = slice(lead + n * chunk, lead + (n + 1) * chunk)
+        at, size = chunk[n]
+        sl = slice(at, at + size)
+        sh = slice(lead + at, lead + at + size)
         b_copy(n).wait_recv()
         if n == 0:
             coup = (
@@ -602,18 +681,18 @@
             gain_col[sl, :] * normed - xin[sl, :].astype(F32) * drag
         )
         res[sl, :] = val.astype(BF)
-        x_copy(n).start()
-
-    for n in range(parts):
-        ag_cross(n).wait_send()
-        ag_fwd(n).wait_send()
-    ag_part.wait_send()
+        x_copy(at, size).start()
+
+    shards = gath.at[pl.ds(0, 3)]
+    remote(shards, shards, ag_s, ag_r.at[0], {"tp": partner}).wait_send()
     for d in range(1, reach + 1):
 
         @pl.when(sends_up(d))
         def _():
-            k_copy(d).wait_send()
-            v_copy(d).wait_send()
+            both_blocks = kb.at[pl.ds(0, 2 * rows)]
+            remote(
+                both_blocks, both_blocks, kv_s.at[d - 1], k_r.at[d - 1], {"ctx": i + 1}
+            ).wait_send()
 
     for n in range(len(far)):
 
@@ -621,23 +700,20 @@
         def _():
             q_copy(n).wait_send()
             stat_copy(n).wait_send()
-            for g in range(kv_heads):
-                do_copy(n, g).wait_send()
+            remote(
+                do_t, do_far.at[n], do_s.at[n], do_r.at[n, 0], {"ctx": i - far[n]}
+            ).wait_send()
 
     if reach >= 1:
 
-        @pl.when(has_down)
-        def _():
-            for g in range(kv_heads):
-                acc_copy(g).wait_send()
+        @pl.when(sends_acc)
+        def _():
+            remote(snd, rcv, acc_s, acc_r.at[0], {"ctx": i - 1}).wait_send()
 
     send_c.wait_send()
-    for m in range(len(groups)):
-        a_copy(m).wait_send()
-    for n in range(chunks):
-        b_copy(n).wait_send()
-    for n in range(chunks):
-        x_copy(n).wait()
+    remote(rs_a, rs_ar, rs_s.at[0], rs_rv.at[1], {"tp": partner}).wait_send()
+    remote(rs_b, rs_br, rs_s.at[2], rs_rv.at[base], {"tp": cross}).wait_send()
+    x_copy(0, width).wait()
 
 
 def per_device(up, xin, inv, gain, q, k, v, ao, wq, wk, wv, wo, lens):
@@ -652,7 +728,7 @@
     kv_cols, q_cols = k.shape[1], q.shape[1]
     kv_heads = kv_cols // HEAD_SIZE
     stacked = rows * (q_cols // kv_cols)
-    chunks = chunk_count(width)
+    chunks = len(chunk_cuts(width))
     groups = len(chunk_groups(chunks))
     parts = len(gather_cuts(width))
     vm = pltpu.VMEM
@@ -688,9 +764,10 @@
         vm((far, kv_heads, HEAD_SIZE, stacked), BF),
         vm((far, kv_heads, HEAD_SIZE, stacked), BF),
         vm((far, stats, stacked), F32),
-        vm((far, kv_heads, rows, stacked), F32),
+        vm((far, kv_heads, 2 * rows, stacked), F32),
         vm((kv_heads, own * rows, HEAD_SIZE), F32),
         vm((kv_heads, own * rows, HEAD_SIZE), F32),
+        vm((q_cols, rows), BF),
         vm((kv_heads, 2 * rows, HEAD_SIZE), BF),
         vm((kv_heads, 2 * rows, HEAD_SIZE), BF),
         vm((tp_n, width, rows), F32),
@@ -698,19 +775,24 @@
     scratch += [vm((COUPLING_ROWS + width, rows), BF)] * 6
     scratch += [vm((width, rows), BF)]
     scratch += [dma((13,))]
-    scratch += [dma((blocks,))] * 4
-    scratch += [dma((2 * parts + 1,))] * 2
+    scratch += [dma((max(reach, 1),))] * 3
+    scratch += [dma(())]
+    scratch += [dma((2 * parts + 1,))]
     scratch += [dma((far,))] * 2
-    scratch += [dma((far, kv_heads))] * 2
+    scratch += [dma((far,))]
+    scratch += [dma((far, kv_heads))]
     scratch += [dma((far,))] * 2
-    scratch += [dma((kv_heads,))] * 2
-    scratch += [dma((1 + groups + chunks,))] * 2
-    scratch += [dma((chunks,))] * 2
+    scratch += [dma(())]
+    scratch += [dma((kv_heads,))]
+    scratch += [pltpu.SemaphoreType.REGULAR] * 2
+    scratch += [dma((3,))]
+    scratch += [dma((1 + groups + chunks,))]
+    scratch += [dma(())] * 2
     out = pl.pallas_call(
         functools.partial(kernel, ctx_n, pipe_n, reach),
-        out_shape=jax.ShapeDtypeStruct((width, rows), BF),
+        out_shape=vm((width, rows), BF),
         in_specs=[pl.BlockSpec(memory_space=pl.ANY)] * 13,
-        out_specs=pl.BlockSpec(memory_space=pl.ANY),
+        out_specs=pl.BlockSpec(memory_space=vm),
         scratch_shapes=scratch,
         compiler_params=pltpu.CompilerParams(collective_id=0, has_side_effects=True),
         name="layer_backward",

time: 36.8 us -> 34.3 us (0.932)
  Pallas kernels: 34.4 us -> 32.8 us
  local copies, waits for them, and re-layouts: 1.6 us -> 0.67 us
    pallas_call x1, Pallas kernels: 34.4 us -> 32.8 us  [per_device(): pl.pallas_call(functools.partial(kernel, ctx_n, pipe_n, reach), out_shape...]
    unnamed x1, local copies, waits for them, and re-layouts: 1.6 us -> 0.67 us
where the time goes in v2:
time: 34.3 us; the launch traced here: 34.1 us
  Pallas kernels  32.8 us (96%)
  local copies, waits for them, and re-layouts  0.67 us (2%)
  between operations  0.66 us (2%)
    pallas_call x1, Pallas kernels, per_device(): pl.pallas_call(functools.partial(kernel, ctx_n, pipe_n, reach), out_shape...  32.8 us

profile of v2, /device:TPU:0, one launch (start us, length us, event | category | flops | bytes accessed | tf_op | source)
XLA Modules:
  0.0 34.1 jit_solution(13903424219904133585)
XLA Ops:
  0.7 32.8 %layer_backward.1 = bf16[672,128]{1,0:T(8,128)(2,1)S(1)} custom-call(bf16[672,128]{1,0:T(8,128)(2,1)} %bitcast.22, bf16[672,128]{1,0:T(8,128)(2,1)} %bitcast.23, f32[1,128]{1,0:T(1,128)} %inv_h.1, f32[1,672]{1,0:T(1,128)} %gain_h.1, bf16[128,512]{1,0:T(8,128)(2,1)} %bitcast.24, bf16[128,256]{1,0:T(8,128)(2,1)} %bitcast.26, bf16[128,256]{1,0:T(8,128)(2,1)} %bitcast.27, ...), custom_call_target="tpu_custom_call" | custom-call | tf_op jit(solution)/shard_map/layer_backward/pallas_call | solution.py:791
  33.5 0.7 %copy.15 = bf16[1,128,672]{1,2,0:T(8,128)(2,1)} copy(bf16[1,128,672]{1,2,0:T(8,128)(2,1)S(1)} %bitcast.17) | data formatting | bytes 344064

commit v3 on v2

--- a/solution.py
+++ b/solution.py
@@ -14,8 +14,7 @@
 QUERY_SCALAR = 168
 NEG_FILL = -1e30
 GATHER_ROWS = 256
-CHUNK_ROWS = 128
-CHUNK_TAIL = 64
+CHUNK_ROWS = 64
 COUPLING_ROWS = 16
 NT = (((1,), (1,)), ((), ()))
 NN = (((1,), (0,)), ((), ()))
@@ -25,14 +24,7 @@
 
 
 def chunk_cuts(width):
-    cuts, at = [], 0
-    while width - at > CHUNK_ROWS + CHUNK_TAIL // 2:
-        cuts.append((at, CHUNK_ROWS))
-        at += CHUNK_ROWS
-    if width - at > CHUNK_TAIL:
-        cuts.append((at, width - at - CHUNK_TAIL))
-        at = width - CHUNK_TAIL
-    return cuts + [(at, width - at)]
+    return [(at, min(CHUNK_ROWS, width - at)) for at in range(0, width, CHUNK_ROWS)]
 
 
 def gather_cuts(width):
@@ -40,12 +32,8 @@
 
 
 def chunk_groups(chunks):
-    groups, first, count = [], 0, 1
-    while first < chunks:
-        count = min(count, chunks - first)
-        groups.append((first, count))
-        first, count = first + count, count + 1
-    return groups
+    edges = sorted({0, min(1, chunks), min(4, chunks), chunks})
+    return [(a, b - a) for a, b in zip(edges, edges[1:])]
 
 
 def direct_reach(reach):
@@ -87,8 +75,7 @@
     vb,
     ao,
     wq,
-    wk,
-    wv,
+    wkv,
     wo,
     slen,
     wo_cut,
@@ -108,6 +95,8 @@
     part_v,
     part_k,
     dq_low,
+    dkv,
+    v_t,
     snd,
     rcv,
     pacc,
@@ -147,7 +136,8 @@
     diag = 3 - t
     rows = q.shape[0]
     width = xin.shape[0]
-    kv_heads = kb.shape[1] // HEAD_SIZE
+    kv_cols = kb.shape[1]
+    kv_heads = kv_cols // HEAD_SIZE
     group = q.shape[1] // kb.shape[1]
     stacked = group * rows
     scale = QUERY_SCALAR ** (-0.5)
@@ -214,8 +204,8 @@
     c_gain = local(gain_h, gain, 12)
     c_v = local(v_h, vb.at[pl.ds(0, rows)], 4)
     c_wq = local(wq_h, wq, 7)
-    c_wk = local(wk_h, wk, 8)
-    c_wv = local(wv_h, wv, 9)
+    c_wk = local(wk_h, wkv.at[:, pl.ds(0, kv_cols)], 8)
+    c_wv = local(wv_h, wkv.at[:, pl.ds(kv_cols, kv_cols)], 9)
     c_xin = local(xin_h, xin, 10)
     c_inv = local(inv_h, inv, 11)
 
@@ -285,6 +275,10 @@
             gath.at[cross, sl], gath.at[cross, sl], ag_s, ag_r.at[m], {"tp": partner}
         )
 
+    last = pl.ds(*cuts[-1])
+    ag_twin = remote(
+        up_h.at[last], gath.at[t, last], ag_s, ag_r.at[2 * parts - 1], {"tp": diag}
+    )
     ag_part = remote(
         up_h, gath.at[t], ag_s, ag_r.at[2 * parts], {"tp": partner}
     )
@@ -314,6 +308,7 @@
         relay(0)
     for n in range(parts):
         ag_cross(n).start()
+    first_core = t % 2 == 0
     if reach >= 1:
 
         @pl.when(has_up)
@@ -371,14 +366,26 @@
     c_ao.wait()
     for h in range(kv_heads * group):
         ao_t[head_cols(h), :] = flip(ao[:, head_cols(h)])
+    c_v.wait()
+    for g in range(kv_heads):
+        v_t[g] = flip(vb[:rows, head_cols(g)])
     c_gain.wait()
     gain_col[...] = jnp.broadcast_to(gain[...], (rows, width)).T
     if reach >= 3:
         relay(1)
 
+    def shard_dot(owner, n):
+        at, size = cuts[n]
+        return dot(wo_cut[owner, :, at : at + size], gath[owner, at : at + size], NN)
+
     c_up.wait()
     acc = dot(wo_cut[t], gath[t], NN)
     ag_part.wait_recv()
+
+    @pl.when(first_core)
+    def _():
+        ag_twin.start()
+
     acc = acc + dot(wo_cut[partner], gath[partner], NN)
 
     for step in range(2, reach):
@@ -412,22 +419,19 @@
         pass_on(k_copy)
         scores(1)
 
-    def shard_dot(owner, n):
-        at, size = cuts[n]
-        return dot(wo_cut[owner, :, at : at + size], gath[owner, at : at + size], NN)
-
     for n in range(parts):
         ag_cross(n).wait_recv()
-        ag_fwd(n).start()
+        if n + 1 < parts:
+            ag_fwd(n).start()
+        else:
+            pl.when(jnp.logical_not(first_core))(ag_fwd(n).start)
         acc = acc + shard_dot(cross, n)
-        if n > 0:
-            ag_fwd(n - 1).wait_recv()
-            acc = acc + shard_dot(diag, n - 1)
-    if reach >= 1:
-        take(v_copy, 1)
-        pass_on(v_copy)
-    ag_fwd(parts - 1).wait_recv()
-    acc = acc + shard_dot(diag, parts - 1)
+    for n in range(parts):
+        if n + 1 == parts and reach >= 1:
+            take(v_copy, 1)
+            pass_on(v_copy)
+        ag_fwd(n).wait_recv()
+        acc = acc + shard_dot(diag, n)
     grad = acc.astype(BF)
     for g in range(kv_heads):
         for r in range(group):
@@ -488,24 +492,23 @@
         def _():
             v_copy(d).start()
 
-    c_v.wait()
     for d in range(2, reach + 1):
         take(v_copy, d)
 
     own = min(reach, 1) + 1
     for g in range(kv_heads):
         dp[g] = dot(vb[:, head_cols(g)], do_t[g], NN)
-        part_v[g] = dot(s[g, : own * rows].astype(BF), do_t[g], NT)
+        part_v[g] = dot(do_t[g], s[g, : own * rows].astype(BF), NT)
         delta = stat[3 * g + 2 : 3 * g + 3, :]
         for d in range(reach + 1):
             ds[g, block_rows(d)] = (
                 s[g, block_rows(d)] * (dp[g, block_rows(d)] - delta)
             ).astype(BF)
-        part_k[g] = dot(ds[g, : own * rows], q_t[g], NT)
+        part_k[g] = dot(q_t[g], ds[g, : own * rows], NT)
 
     def send_acc(g):
-        snd[g, :rows] = part_v[g, block_rows(1)].astype(BF)
-        snd[g, rows:] = part_k[g, block_rows(1)].astype(BF)
+        snd[g, :HEAD_SIZE] = part_v[g, :, block_rows(1)].astype(BF)
+        snd[g, HEAD_SIZE:] = part_k[g, :, block_rows(1)].astype(BF)
         acc_copy(g).start()
 
     if reach == 1:
@@ -519,8 +522,8 @@
 
         @pl.when(i != 1)
         def _():
-            part_v[:, block_rows(1)] = jnp.zeros((kv_heads, rows, HEAD_SIZE), F32)
-            part_k[:, block_rows(1)] = jnp.zeros((kv_heads, rows, HEAD_SIZE), F32)
+            part_v[:, :, block_rows(1)] = jnp.zeros((kv_heads, HEAD_SIZE, rows), F32)
+            part_k[:, :, block_rows(1)] = jnp.zeros((kv_heads, HEAD_SIZE, rows), F32)
 
     coupling = jnp.zeros((1, rows), F32)
     low = []
@@ -567,10 +570,10 @@
                 do_copy(n, g).wait_recv()
                 for at, (kd, _) in enumerate(far_blocks(n)):
                     pr = s_far[n, g, block_rows(at)]
-                    part_v[g, block_rows(kd)] += dot(pr.astype(BF), do_far[n, g], NT)
+                    part_v[g, :, block_rows(kd)] += dot(do_far[n, g], pr.astype(BF), NT)
                     dprob = dot(vb[block_rows(kd), head_cols(g)], do_far[n, g], NN)
                     dsc = (pr * (dprob - delta)).astype(BF)
-                    part_k[g, block_rows(kd)] += dot(dsc, q_far[n, g], NT)
+                    part_k[g, :, block_rows(kd)] += dot(q_far[n, g], dsc, NT)
                     if kd == 1:
                         send_acc(g)
 
@@ -601,21 +604,19 @@
         def _():
             for g in range(kv_heads):
                 acc_copy(g).wait_recv()
-                part_v[g, :rows] += rcv[g, :rows].astype(F32)
-                part_k[g, :rows] += rcv[g, rows:].astype(F32)
-
-    dv_low = jnp.concatenate([part_v[g, :rows].astype(BF) for g in range(kv_heads)], axis=1)
-    dk_low = jnp.concatenate(
-        [(part_k[g, :rows] * scale).astype(BF) for g in range(kv_heads)], axis=1
-    )
-    both = dk_low.astype(F32) * kb[:rows].astype(F32) + dv_low.astype(F32) * vb[:rows].astype(F32)
+                part_v[g, :, :rows] += rcv[g, :HEAD_SIZE].astype(F32)
+                part_k[g, :, :rows] += rcv[g, HEAD_SIZE:].astype(F32)
+
     for g in range(kv_heads):
-        coupling = coupling + jnp.sum(both[:, head_cols(g)].T, axis=0, keepdims=True)
+        dk_low = (part_k[g, :, :rows] * scale).astype(BF)
+        dv_low = part_v[g, :, :rows].astype(BF)
+        dkv[head_cols(g), :] = dk_low
+        dkv[head_cols(kv_heads + g), :] = dv_low
+        both = dk_low.astype(F32) * k_t[g, :, :rows].astype(F32) + dv_low.astype(F32) * v_t[g]
+        coupling = coupling + jnp.sum(both, axis=0, keepdims=True)
 
     def piece(n, at=0, size=width):
-        span = piece_rows(n, at, size)
-        more = dot(wk[span, :], dk_low, NT) + dot(wv[span, :], dv_low, NT)
-        return pacc[n, at : at + size] + more
+        return pacc[n, at : at + size] + dot(wkv[piece_rows(n, at, size), :], dkv[...], NN)
 
     lead = COUPLING_ROWS
     wide = jnp.broadcast_to(coupling, (lead, rows))
@@ -747,8 +748,7 @@
         vm((blocks * rows, kv_cols), BF),
         vm(ao.shape, BF),
         vm(wq.shape, BF),
-        vm(wk.shape, BF),
-        vm(wv.shape, BF),
+        vm((wk.shape[0], 2 * kv_cols), BF),
         vm(wo.shape, BF),
         pltpu.SMEM(lens.shape, jnp.int32),
         vm((tp_n, wo.shape[0], width), BF),
@@ -765,11 +765,13 @@
         vm((far, kv_heads, HEAD_SIZE, stacked), BF),
         vm((far, stats, stacked), F32),
         vm((far, kv_heads, 2 * rows, stacked), F32),
-        vm((kv_heads, own * rows, HEAD_SIZE), F32),
-        vm((kv_heads, own * rows, HEAD_SIZE), F32),
+        vm((kv_heads, HEAD_SIZE, own * rows), F32),
+        vm((kv_heads, HEAD_SIZE, own * rows), F32),
         vm((q_cols, rows), BF),
-        vm((kv_heads, 2 * rows, HEAD_SIZE), BF),
-        vm((kv_heads, 2 * rows, HEAD_SIZE), BF),
+        vm((2 * kv_cols, rows), BF),
+        vm((kv_heads, HEAD_SIZE, rows), F32),
+        vm((kv_heads, 2 * HEAD_SIZE, rows), BF),
+        vm((kv_heads, 2 * HEAD_SIZE, rows), BF),
         vm((tp_n, width, rows), F32),
     ]
     scratch += [vm((COUPLING_ROWS + width, rows), BF)] * 6

time: 34.3 us -> 33.8 us (0.985)
  Pallas kernels: 32.8 us -> 32.3 us
    pallas_call x1, Pallas kernels: 32.8 us -> 32.3 us  [per_device(): pl.pallas_call(functools.partial(kernel, ctx_n, pipe_n, reach), out_shape...]
where the time goes in v3:
time: 33.8 us; the launch traced here: 33.7 us
  Pallas kernels  32.3 us (96%)
  local copies, waits for them, and re-layouts  0.67 us (2%)
  between operations  0.66 us (2%)
    pallas_call x1, Pallas kernels, per_device(): pl.pallas_call(functools.partial(kernel, ctx_n, pipe_n, reach), out_shape...  32.3 us

profile of v3, /device:TPU:0, one launch (start us, length us, event | category | flops | bytes accessed | tf_op | source)
XLA Modules:
  0.0 33.7 jit_solution(6987530593866992863)
XLA Ops:
  0.7 32.3 %layer_backward.1 = bf16[672,128]{1,0:T(8,128)(2,1)S(1)} custom-call(bf16[672,128]{1,0:T(8,128)(2,1)} %bitcast.22, bf16[672,128]{1,0:T(8,128)(2,1)} %bitcast.23, f32[1,128]{1,0:T(1,128)} %inv_h.1, f32[1,672]{1,0:T(1,128)} %gain_h.1, bf16[128,512]{1,0:T(8,128)(2,1)} %bitcast.24, bf16[128,256]{1,0:T(8,128)(2,1)} %bitcast.26, bf16[128,256]{1,0:T(8,128)(2,1)} %bitcast.27, ...), custom_call_target="tpu_custom_call" | custom-call | tf_op jit(solution)/shard_map/layer_backward/pallas_call | solution.py:793
  33.0 0.7 %copy.15 = bf16[1,128,672]{1,2,0:T(8,128)(2,1)} copy(bf16[1,128,672]{1,2,0:T(8,128)(2,1)S(1)} %bitcast.17) | data formatting | bytes 344064

commit v4 on v3

--- a/solution.py
+++ b/solution.py
@@ -32,7 +32,7 @@
 
 
 def chunk_groups(chunks):
-    edges = sorted({0, min(1, chunks), min(4, chunks), chunks})
+    edges = sorted({1, min(4, chunks), chunks})
     return [(a, b - a) for a, b in zip(edges, edges[1:])]
 
 
@@ -106,6 +106,8 @@
     rs_br,
     rs_c,
     rs_cr,
+    rs_d,
+    rs_dr,
     res,
     lsem,
     kv_s,
@@ -119,13 +121,10 @@
     do_r,
     st_s,
     st_r,
-    acc_s,
     acc_r,
     from_low,
     from_high,
-    rs_s,
     rs_rv,
-    x_s,
     x_r,
 ):
     i = lax.axis_index("ctx")
@@ -260,7 +259,7 @@
         takes_acc = has_up
 
     def acc_copy(g):
-        return remote(snd.at[g], rcv.at[g], acc_s, acc_r.at[g], {"ctx": i - 1})
+        return remote(snd.at[g], rcv.at[g], lsem.at[5], acc_r.at[g], {"ctx": i - 1})
 
     parts = len(cuts)
 
@@ -629,41 +628,52 @@
 
     def a_copy(m):
         sl = pl.ds(*span_of(*groups[m]))
-        return remote(rs_a.at[sl], rs_ar.at[sl], rs_s.at[0], rs_rv.at[1 + m], {"tp": partner})
-
-    send_c = remote(rs_c, rs_cr, rs_s.at[1], rs_rv.at[0], {"tp": partner})
+        return remote(rs_a.at[sl], rs_ar.at[sl], lsem.at[0], rs_rv.at[1 + m], {"tp": partner})
+
+    send_c = remote(rs_c, rs_cr, lsem.at[1], rs_rv.at[0], {"tp": partner})
     base = 1 + len(groups)
+    head = chunk[0][1]
+    send_d = remote(rs_d, rs_dr, lsem.at[6], rs_rv.at[base + chunks], {"tp": diag})
 
     def b_copy(n):
         sl = pl.ds(*span_of(n))
-        return remote(rs_b.at[sl], rs_br.at[sl], rs_s.at[2], rs_rv.at[base + n], {"tp": cross})
+        return remote(rs_b.at[sl], rs_br.at[sl], lsem.at[3], rs_rv.at[base + n], {"tp": cross})
 
     def x_copy(at, size):
         sl = pl.ds(at, size)
         if pipe_n == 1:
-            return pltpu.make_async_copy(res.at[sl], out_h.at[sl], x_s)
-        return remote(res.at[sl], out_h.at[sl], x_s, x_r, {"pipe": prev})
-
-    rs_a[:lead, :] = wide.astype(BF)
-    for m, (first, count) in enumerate(groups):
+            return pltpu.make_async_copy(res.at[sl], out_h.at[sl], lsem.at[12])
+        return remote(res.at[sl], out_h.at[sl], lsem.at[12], x_r, {"pipe": prev})
+
+    def send_a(m):
+        first, count = groups[m]
         at, size = chunk[first][0], sum(chunk[n][1] for n in range(first, first + count))
         rs_a[lead + at : lead + at + size, :] = piece(0, at, size).astype(BF)
         a_copy(m).start()
+
+    send_a(0)
+    rs_d[:lead, :] = wide.astype(BF)
+    rs_d[lead:, :] = piece(0, 0, head).astype(BF)
+    send_d.start()
+    rs_b[:lead, :] = wide.astype(BF)
+    rs_b[lead : lead + head, :] = piece(1, 0, head).astype(BF)
+    b_copy(0).start()
+    for m in range(1, len(groups)):
+        send_a(m)
     for m, (first, count) in enumerate(groups):
         at, size = chunk[first][0], sum(chunk[n][1] for n in range(first, first + count))
         pacc[1, at : at + size] = piece(1, at, size)
         a_copy(m).wait_recv()
-        if m == 0:
-            rs_b[:lead, :] = (wide + rs_ar[:lead, :].astype(F32)).astype(BF)
         for n in range(first, first + count):
             at, size = chunk[n]
             sl = slice(at, at + size)
             sh = slice(lead + at, lead + at + size)
             rs_b[sh, :] = (pacc[1, sl] + rs_ar[sh, :].astype(F32)).astype(BF)
             b_copy(n).start()
-    rs_c[lead:, :] = piece(2).astype(BF)
-    rs_c[:lead, :] = wide.astype(BF)
-    send_c.start()
+        if m == 0:
+            rs_c[lead:, :] = piece(2).astype(BF)
+            rs_c[:lead, :] = wide.astype(BF)
+            send_c.start()
     pacc[3] = piece(3)
     iv = inv[...]
     send_c.wait_recv()
@@ -672,12 +682,13 @@
         sl = slice(at, at + size)
         sh = slice(lead + at, lead + at + size)
         b_copy(n).wait_recv()
+        normed = pacc[3, sl] + rs_cr[sh, :].astype(F32) + rs_br[sh, :].astype(F32)
         if n == 0:
-            coup = (
-                coupling + rs_cr[:lead, :].astype(F32)[:1] + rs_br[:lead, :].astype(F32)[:1]
-            )
+            send_d.wait_recv()
+            coup = coupling + rs_cr[:lead, :].astype(F32)[:1]
+            coup = coup + rs_br[:lead, :].astype(F32)[:1] + rs_dr[:lead, :].astype(F32)[:1]
             drag = iv * coup / model_width
-        normed = pacc[3, sl] + rs_cr[sh, :].astype(F32) + rs_br[sh, :].astype(F32)
+            normed = normed + rs_dr[lead:, :].astype(F32)
         val = gath[t, sl, :].astype(F32) + iv * (
             gain_col[sl, :] * normed - xin[sl, :].astype(F32) * drag
         )
@@ -709,11 +720,15 @@
 
         @pl.when(sends_acc)
         def _():
-            remote(snd, rcv, acc_s, acc_r.at[0], {"ctx": i - 1}).wait_send()
+            remote(snd, rcv, lsem.at[5], acc_r.at[0], {"ctx": i - 1}).wait_send()
 
     send_c.wait_send()
-    remote(rs_a, rs_ar, rs_s.at[0], rs_rv.at[1], {"tp": partner}).wait_send()
-    remote(rs_b, rs_br, rs_s.at[2], rs_rv.at[base], {"tp": cross}).wait_send()
+    send_d.wait_send()
+    rest = pl.ds(lead + head, width - head)
+    remote(
+        rs_a.at[rest], rs_ar.at[rest], lsem.at[0], rs_rv.at[1], {"tp": partner}
+    ).wait_send()
+    remote(rs_b, rs_br, lsem.at[3], rs_rv.at[base], {"tp": cross}).wait_send()
     x_copy(0, width).wait()
 
 
@@ -775,6 +790,7 @@
         vm((tp_n, width, rows), F32),
     ]
     scratch += [vm((COUPLING_ROWS + width, rows), BF)] * 6
+    scratch += [vm((COUPLING_ROWS + chunk_cuts(width)[0][1], rows), BF)] * 2
     scratch += [vm((width, rows), BF)]
     scratch += [dma((13,))]
     scratch += [dma((max(reach, 1),))] * 3
@@ -784,12 +800,10 @@
     scratch += [dma((far,))]
     scratch += [dma((far, kv_heads))]
     scratch += [dma((far,))] * 2
-    scratch += [dma(())]
     scratch += [dma((kv_heads,))]
     scratch += [pltpu.SemaphoreType.REGULAR] * 2
-    scratch += [dma((3,))]
-    scratch += [dma((1 + groups + chunks,))]
-    scratch += [dma(())] * 2
+    scratch += [dma((2 + groups + chunks,))]
+    scratch += [dma(())]
     out = pl.pallas_call(
         functools.partial(kernel, ctx_n, pipe_n, reach),
         out_shape=vm((width, rows), BF),

time: 33.8 us -> 33.5 us (level)
    pallas_call x1, Pallas kernels: 32.3 us -> 32 us  [per_device(): pl.pallas_call(functools.partial(kernel, ctx_n, pipe_n, reach), out_shape...]
where the time goes in v4:
time: 33.5 us; the launch traced here: 33.3 us
  Pallas kernels  32 us (96%)
  local copies, waits for them, and re-layouts  0.67 us (2%)
  between operations  0.66 us (2%)
    pallas_call x1, Pallas kernels, per_device(): pl.pallas_call(functools.partial(kernel, ctx_n, pipe_n, reach), out_shape...  32 us
    unnamed x1, local copies, waits for them, and re-layouts  0.67 us

profile of v4, /device:TPU:0, one launch (start us, length us, event | category | flops | bytes accessed | tf_op | source)
XLA Modules:
  0.0 33.3 jit_solution(16760741338378672706)
XLA Ops:
  0.7 32.0 %layer_backward.1 = bf16[672,128]{1,0:T(8,128)(2,1)S(1)} custom-call(bf16[672,128]{1,0:T(8,128)(2,1)} %bitcast.22, bf16[672,128]{1,0:T(8,128)(2,1)} %bitcast.23, f32[1,128]{1,0:T(1,128)} %inv_h.1, f32[1,672]{1,0:T(1,128)} %gain_h.1, bf16[128,512]{1,0:T(8,128)(2,1)} %bitcast.24, bf16[128,256]{1,0:T(8,128)(2,1)} %bitcast.26, bf16[128,256]{1,0:T(8,128)(2,1)} %bitcast.27, ...), custom_call_target="tpu_custom_call" | custom-call | tf_op jit(solution)/shard_map/layer_backward/pallas_call | solution.py:807
  32.6 0.7 %copy.15 = bf16[1,128,672]{1,2,0:T(8,128)(2,1)} copy(bf16[1,128,672]{1,2,0:T(8,128)(2,1)S(1)} %bitcast.17) | data formatting | bytes 344064

commit v5 on v4

--- a/solution.py
+++ b/solution.py
@@ -483,7 +483,7 @@
         for n in range(1, len(far)):
             send_dout(n, range(1))
             send_stat(n)
-        for n in range(len(far)):
+        for n in reversed(range(len(far))):
             send_dout(n, range(1, kv_heads))
     for d in direct[1:]:
 

time: 33.5 us -> 34.5 us (1.030)
  Pallas kernels: 32 us -> 33 us
    pallas_call x1, Pallas kernels: 32 us -> 33 us  [per_device(): pl.pallas_call(functools.partial(kernel, ctx_n, pipe_n, reach), out_shape...]
where the time goes in v5:
time: 34.5 us; the launch traced here: 34.3 us
  Pallas kernels  33 us (96%)
  local copies, waits for them, and re-layouts  0.67 us (2%)
  between operations  0.66 us (2%)
    pallas_call x1, Pallas kernels, per_device(): pl.pallas_call(functools.partial(kernel, ctx_n, pipe_n, reach), out_shape...  33 us

profile of v5, /device:TPU:0, one launch (start us, length us, event | category | flops | bytes accessed | tf_op | source)
XLA Modules:
  0.0 34.3 jit_solution(9721756417741586985)
XLA Ops:
  0.7 33.0 %layer_backward.1 = bf16[672,128]{1,0:T(8,128)(2,1)S(1)} custom-call(bf16[672,128]{1,0:T(8,128)(2,1)} %bitcast.22, bf16[672,128]{1,0:T(8,128)(2,1)} %bitcast.23, f32[1,128]{1,0:T(1,128)} %inv_h.1, f32[1,672]{1,0:T(1,128)} %gain_h.1, bf16[128,512]{1,0:T(8,128)(2,1)} %bitcast.24, bf16[128,256]{1,0:T(8,128)(2,1)} %bitcast.26, bf16[128,256]{1,0:T(8,128)(2,1)} %bitcast.27, ...), custom_call_target="tpu_custom_call" | custom-call | tf_op jit(solution)/shard_map/layer_backward/pallas_call | solution.py:807
  33.7 0.7 %copy.15 = bf16[1,128,672]{1,2,0:T(8,128)(2,1)} copy(bf16[1,128,672]{1,2,0:T(8,128)(2,1)S(1)} %bitcast.17) | data formatting | bytes 344064
